TPU v7x, 512 devices: a whole 4x4x16 slice. The times are simulated.
512 devices in a mesh: group: 4 (over y), lat: 16 (over z_hi, x), lon: 8 (over z_lo, core).
Axes of the slice: x: 4, y: 4, z: 16 (z_hi: 4, z_lo: 4; z = z_hi * 4 + z_lo), core: 2. Of those that a mesh axis runs over, the one named last changes fastest.
Arguments:
- species_amounts: float32 [128, 4, 256, 1024], P('group', None, 'lat', 'lon'), may hold values from -4 to 4
- zonal_cell_fraction: float32 [4, 256, 1024], P('group', 'lat', 'lon'), may hold values from -0.3 to 0.3
- meridional_cell_fraction: float32 [4, 256, 1024], P('group', 'lat', 'lon'), may hold values from -0.3 to 0.3
- updraft_cell_fraction: float32 [4, 256, 1024], P('group', 'lat', 'lon'), may hold values from -0.3 to 0.3
- warmth_anomaly: float32 [4, 256, 1024], P('group', 'lat', 'lon'), may hold values from -2 to 2
- mass_per_volume: float32 [4, 256, 1024], P('group', 'lat', 'lon'), may hold values from 0.5 to 2
- chemistry_iterations: int32 [256, 1024], P('lat', 'lon'), may hold values from 1 to 2, as said below
- companion_species: bfloat16 [512, 128], replicated, may hold values from -0.5 to 0.5
- stoichiometric_rate: bfloat16 [128, 512], replicated, may hold values from -0.25 to 0.25
- heat_yield: float32 [128], replicated, may hold values from -0.5 to 0.5
Outputs:
- tracers_out: float32 [128, 4, 256, 1024], P('group', None, 'lat', 'lon')
- east_out: float32 [4, 256, 1024], P('group', 'lat', 'lon')
- north_out: float32 [4, 256, 1024], P('group', 'lat', 'lon')
- temp_out: float32 [4, 256, 1024], P('group', 'lat', 'lon')
Inputs may be any that keep to these rules, and one draw needn't show every extreme that they name: `chemistry_iterations`: columns at latitude rows 192 and above hold 1 or 2, and the last row holds 2; all other columns hold 1.
All inputs are finite; a program needn't handle non-finite values.
Results may differ from a plain program's by a relative error of at most 0.0011.
Values sent between devices are 32-bit elements; how exact they have to be, the bound alone decides.
A program may use at most 64 MiB of HBM per device.

v0:
```python
import jax
import jax.numpy as jnp
from jax import lax
from jax.sharding import PartitionSpec as P

diffusion = 0.1
pressure = 0.05
chem_step = 0.2
block_cells = 512


def cut_along(value, dim, devices):
    lengths = value.shape
    pieces = value.reshape(*lengths[:dim], devices, lengths[dim] // devices, *lengths[dim + 1 :])
    return jnp.moveaxis(pieces, dim, 0)


def joined_along(pieces, dim):
    lengths = list(pieces.shape[1:])
    lengths[dim] *= pieces.shape[0]
    return jnp.moveaxis(pieces, 0, dim).reshape(lengths)


def one_exchange(value, axis, axes, splits, concats):
    sizes = [lax.axis_size(a) for a in axes]
    pieces = cut_along(value, splits[0], sizes[0])
    pieces = jnp.moveaxis(cut_along(pieces, splits[1] + 1, sizes[1]), 0, 1)
    inside = pieces.shape[2:]
    pieces = pieces.reshape(-1, *inside)
    pieces = lax.all_to_all(pieces, axis, split_axis=0, concat_axis=0, tiled=True)
    pieces = joined_along(pieces.reshape(*sizes, *inside), concats[0] + 1)
    return joined_along(pieces, concats[1])


def extended(value, sides, width):
    edges = {}
    for axis, dim in sides:
        devices, length = (lax.axis_size(axis), value.shape[dim])
        up = [(i, (i + 1) % devices) for i in range(devices - 1)]
        last = lax.slice_in_dim(value, length - width, length, axis=dim)
        leading = lax.slice_in_dim(value, 0, width, axis=dim)
        edges[dim] = (
            lax.ppermute(last, axis, up),
            lax.ppermute(leading, axis, [(b, a) for a, b in up]),
        )
    done = []
    for _, dim in sides:
        low, high = edges[dim]
        around = [(width, width) if d in done else (0, 0) for d in range(value.ndim)]
        value = jnp.concatenate([jnp.pad(low, around), value, jnp.pad(high, around)], axis=dim)
        done.append(dim)
    return value


def transport(padded, east_pad, north_pad, upward):
    zonal_cells = padded[..., 1:-1, :]
    zonal_wind = east_pad[:, 1:-1, :]
    face_wind = 0.5 * (zonal_wind[..., :-1] + zonal_wind[..., 1:])
    face_flux = (
        jnp.maximum(face_wind, 0.0) * zonal_cells[..., :-1]
        + jnp.minimum(face_wind, 0.0) * zonal_cells[..., 1:]
    )
    change = face_flux[..., 1:] - face_flux[..., :-1]
    north_cells = padded[..., 1:-1]
    north_wind = north_pad[:, :, 1:-1]
    face_wind = 0.5 * (north_wind[:, :-1] + north_wind[:, 1:])
    face_flux = (
        jnp.maximum(face_wind, 0.0) * north_cells[..., :-1, :]
        + jnp.minimum(face_wind, 0.0) * north_cells[..., 1:, :]
    )
    change = change + (face_flux[..., 1:, :] - face_flux[..., :-1, :])
    centre = padded[..., 1:-1, 1:-1]
    face_wind = 0.5 * (upward[:-1] + upward[1:])
    face_flux = (
        jnp.maximum(face_wind, 0.0) * centre[..., :-1, :, :]
        + jnp.minimum(face_wind, 0.0) * centre[..., 1:, :, :]
    )
    closed = jnp.zeros_like(face_flux[..., :1, :, :])
    face_flux = jnp.concatenate([closed, face_flux, closed], axis=-3)
    change = change + (face_flux[..., 1:, :, :] - face_flux[..., :-1, :, :])
    return centre - change


def dynamics(padded):
    centre = padded[:, :, 1:-1, 1:-1]
    eastern = padded[:, :, 1:-1, 2:]
    western = padded[:, :, 1:-1, :-2]
    northern = padded[:, :, 2:, 1:-1]
    southern = padded[:, :, :-2, 1:-1]
    laplace = eastern + western + northern + southern - 4.0 * centre
    diffused = centre + diffusion * laplace
    zonal_axis_name = diffused[0] - pressure * (eastern[2] - western[2])
    meridional_axis_name = diffused[1] - pressure * (northern[2] - southern[2])
    return (zonal_axis_name, meridional_axis_name, diffused[2])


def react_block(
    tracer_block, rate_block, count_block, companion_species, stoichiometric_rate, heat_yield
):
    species = tracer_block.shape[0]
    width = tracer_block.shape[1]
    repeats = companion_species.shape[0] // species
    deepest = jnp.max(count_block)

    def keep_going(state_pair):
        return state_pair[0] < deepest

    def substep(state_pair):
        counter, current = state_pair
        narrow = current.astype(jnp.bfloat16)
        pair_terms = jnp.dot(companion_species, narrow, preferred_element_type=jnp.float32)
        quadratic = (
            (pair_terms.reshape(repeats, species, width) * current[None])
            .reshape(repeats * species, width)
            .astype(jnp.bfloat16)
        )
        tendency = (
            rate_block[None]
            * jnp.dot(stoichiometric_rate, quadratic, preferred_element_type=jnp.float32)
            - current
        )
        current = jnp.where(counter < count_block[None], current + chem_step * tendency, current)
        return (counter + 1, current)

    final = lax.while_loop(keep_going, substep, (jnp.zeros((), jnp.int32), tracer_block))[1]
    heating = jnp.dot(heat_yield[None], final - tracer_block, precision=lax.Precision.HIGHEST)[0]
    return (final, heating)


def react_cells(
    tracer_cells, rate_cells, count_cells, companion_species, stoichiometric_rate, heat_yield
):
    cell_count = tracer_cells.shape[1]
    sort_order = jnp.argsort(-count_cells, stable=True)
    inverse = jnp.argsort(sort_order)
    sorted_tracers = jnp.take(tracer_cells, sort_order, axis=1)
    sorted_rates = jnp.take(rate_cells, sort_order)
    sorted_counts = jnp.take(count_cells, sort_order)

    def one_block(block_index, outputs):
        offset = block_index * block_cells
        tracer_block = lax.dynamic_slice_in_dim(sorted_tracers, offset, block_cells, 1)
        rate_block = lax.dynamic_slice_in_dim(sorted_rates, offset, block_cells, 0)
        count_block = lax.dynamic_slice_in_dim(sorted_counts, offset, block_cells, 0)
        final, heating = react_block(
            tracer_block,
            rate_block,
            count_block,
            companion_species,
            stoichiometric_rate,
            heat_yield,
        )
        return (
            lax.dynamic_update_slice_in_dim(outputs[0], final, offset, 1),
            lax.dynamic_update_slice_in_dim(outputs[1], heating, offset, 0),
        )

    reacted, heated = lax.fori_loop(
        0,
        cell_count // block_cells,
        one_block,
        (jnp.zeros_like(sorted_tracers), jnp.zeros_like(sorted_rates)),
    )
    return (jnp.take(reacted, inverse, axis=1), jnp.take(heated, inverse))


def scattered(
    advected,
    reaction_rate,
    chemistry_iterations,
    companion_species,
    stoichiometric_rate,
    heat_yield,
):
    groups = lax.axis_size("group")
    own_group = lax.axis_index("group")
    stratum_total = advected.shape[1]
    meridian_span = advected.shape[2]
    parallel_span = advected.shape[3]
    column_part = parallel_span // groups
    count_field = jnp.broadcast_to(
        chemistry_iterations.astype(jnp.float32)[None],
        (stratum_total, meridian_span, parallel_span),
    )
    own_rates = lax.dynamic_slice_in_dim(reaction_rate, own_group * column_part, column_part, 2)
    own_counts = lax.dynamic_slice_in_dim(count_field, own_group * column_part, column_part, 2)
    cell_info = jnp.concatenate([own_rates, own_counts], axis=2)[None, :, None]
    arrived, info_in = (
        one_exchange(advected[:, :, None], ("group", "lat"), ("group", "lat"), (1, 3), (0, 2)),
        one_exchange(cell_info, ("group", "lat"), ("group", "lat"), (1, 3), (0, 2)),
    )
    species = arrived.shape[0]
    cell_shape = arrived.shape[1:]
    cell_data = info_in.reshape(groups, cell_shape[0], cell_shape[1], cell_shape[2], 2, column_part)
    cell_data = cell_data.transpose(4, 1, 2, 3, 0, 5).reshape(2, -1)
    reacted, heating = react_cells(
        arrived.reshape(species, -1),
        cell_data[0],
        cell_data[1].astype(jnp.int32),
        companion_species,
        stoichiometric_rate,
        heat_yield,
    )
    heat_copies = jnp.broadcast_to(heating.reshape((1,) + cell_shape), (groups,) + cell_shape)
    returned, heat_back = (
        one_exchange(
            reacted.reshape(arrived.shape), ("group", "lat"), ("group", "lat"), (0, 2), (1, 3)
        ),
        one_exchange(heat_copies, ("group", "lat"), ("group", "lat"), (0, 2), (1, 3)),
    )
    return (returned[:, :, 0], heat_back[0, :, 0])


def local(
    species_amounts,
    zonal_cell_fraction,
    meridional_cell_fraction,
    updraft_cell_fraction,
    warmth_anomaly,
    mass_per_volume,
    chemistry_iterations,
    companion_species,
    stoichiometric_rate,
    heat_yield,
):
    own_group = lax.axis_index("group")
    local_strata = warmth_anomaly.shape[0]
    owned_tracers = species_amounts.shape[0]
    columns = lax.all_gather(
        jnp.stack(
            [
                zonal_cell_fraction,
                meridional_cell_fraction,
                updraft_cell_fraction,
                warmth_anomaly,
                mass_per_volume,
            ]
        ),
        "group",
        axis=1,
        tiled=True,
    )
    zonal_axis_name, meridional_axis_name, upward, heat_snapshot, air_density = (
        columns[0],
        columns[1],
        columns[2],
        columns[3],
        columns[4],
    )
    stacked = jnp.concatenate(
        [species_amounts, jnp.stack([zonal_axis_name, meridional_axis_name, heat_snapshot])], axis=0
    )
    padded = extended(stacked, (("lat", 2), ("lon", 3)), 1)
    advected = transport(
        padded[:owned_tracers], padded[owned_tracers], padded[owned_tracers + 1], upward
    )
    new_east, new_north, warmed = dynamics(padded[owned_tracers:])
    reaction_rate = jax.nn.sigmoid(2.0 * heat_snapshot)
    reacted, heating = scattered(
        advected,
        reaction_rate,
        chemistry_iterations,
        companion_species,
        stoichiometric_rate,
        heat_yield,
    )
    heat_snapshot = warmed + heating / air_density
    start_level = own_group * local_strata
    east_mine = lax.dynamic_slice_in_dim(new_east, start_level, local_strata, 0)
    north_mine = lax.dynamic_slice_in_dim(new_north, start_level, local_strata, 0)
    thermal_mine = lax.dynamic_slice_in_dim(heat_snapshot, start_level, local_strata, 0)
    return (reacted, east_mine, north_mine, thermal_mine)


def solution(mesh):
    return jax.shard_map(
        local,
        mesh=mesh,
        in_specs=(
            P("group", None, "lat", "lon"),
            P("group", "lat", "lon"),
            P("group", "lat", "lon"),
            P("group", "lat", "lon"),
            P("group", "lat", "lon"),
            P("group", "lat", "lon"),
            P("lat", "lon"),
            P(),
            P(),
            P(),
        ),
        out_specs=(
            P("group", None, "lat", "lon"),
            P("group", "lat", "lon"),
            P("group", "lat", "lon"),
            P("group", "lat", "lon"),
        ),
        check_vma=False,
    )
```

profile of v0, /device:TPU:1, one launch (start us, length us, event | category | flops | bytes accessed | tf_op | source)
XLA Modules:
  0.0 285.2 jit_solution(10840602657939708706)
XLA Ops:
  0.6 0.8 constant_dynamic-update-slice_fusion.5
  4.2 10.5 %all_gather.3 = f32[5,4,16,128]{3,2,1,0:T(8,128)S(1)} all-gather(f32[5,1,16,128]{3,2,1,0:T(8,128)S(1)} %constant_dynamic-update-slice_fusion.1), channel_id=1, replica_groups=mesh['group'=4,'lat'=16,'lon'=8] {'group'}, dimensions={1}, use_global_device_ids=true | all-gather | bytes 204800 | tf_op jit(solution)/shard_map/all_gather | solution.py:229
  15.4 0.8 dynamic-slice_convert_fusion
  16.9 20.2 %all-to-all-start.1 = ((f32[64,1,1,1,1,64]{5,4,3,2,1,0:T(1,128)}), f32[64,1,1,1,1,64]{5,4,3,2,1,0:T(1,128)S(1)}, u32[]{:S(2)}, u32[]{:S(2)}) async-start(f32[64,1,1,1,1,64]{5,4,3,2,1,0:T(1,128)} %bitcast.11), calls=%async_computation.1 | async-start | bytes 65536 | tf_op jit(solution)/shard_map/all_to_all | solution.py:30
  37.2 2.0 pad_maximum_fusion.11
  39.1 2.9 %collective-permute-start.1 = (f32[35,4,1,128]{3,2,1,0:T(1,128)}, f32[35,4,1,128]{3,2,1,0:T(1,128)S(1)}, u32[]{:S(2)}, u32[]{:S(2)}) collective-permute-start(f32[35,4,1,128]{3,2,1,0:T(1,128)} %get-tuple-element.257), channel_id=1, source_target_pairs={{0,8},{8,16},{16,24},{24,32},{32,40},{40,48},{48,56},{56,64},{64,7... | collective-permute-start | bytes 215048 | tf_op jit(solution)/shard_map/ppermute | solution.py:43
  42.1 1.3 collective-permute-start.2
  43.9 1.4 copy.90
  45.2 6.3 %collective-permute-start.3 = (f32[35,4,16,1]{0,2,3,1:T(8,128)}, f32[35,4,16,1]{0,2,3,1:T(8,128)S(1)}, u32[]{:S(2)}, u32[]{:S(2)}) collective-permute-start(f32[35,4,16,1]{0,2,3,1:T(8,128)} %copy.90), channel_id=1, source_target_pairs={{1,0},{2,1},{3,2},{4,3},{5,4},{6,5},{7,6},{9,8},{10,9},{11,10},{12... | collective-permute-start | bytes 26888 | tf_op jit(solution)/shard_map/ppermute | solution.py:44
  51.6 0.8 copy.88
  52.3 2.5 collective-permute-start
  54.9 0.8 maximum_bitcast_fusion.1
  55.7 1.0 multiply_add_fusion
  56.7 2.0 copy.89
  58.7 1.5 pad.9
  60.3 2.0 copy.91
  62.3 1.5 pad.10
  63.8 0.9 maximum_bitcast_fusion
  65.0 4.1 %maximum_maximum_fusion = (f32[35,4,18,129]{3,2,1,0:T(8,128)S(1)}, f32[35,4,18,129]{3,2,1,0:T(8,128)S(1)}) fusion(f32[35,4,1,128]{3,2,1,0:T(1,128)} %collective-permute-done.2, f32[1,4,16,128]{3,2,1,0:T(8,128)S(1)} %get-tuple-element.260, f32[2,4,16,128]{3,2,1,0:T(8,128)S(1)} %slice.229, f32[32,4,16,128]{3,2,1,0:T(8,128)S(1)} %copy-done, ...), kind=kLoop, calls=%fused_computation.21 | loop fusion | flops 3250800 | bytes 3911040 | tf_op jit(solution)/shard_map/concatenate | solution.py:50
  69.8 1.3 maximum_maximum_fusion.1
  71.4 0.8 copy-done.8
  72.8 1.6 copy.93
  74.4 22.1 %all-to-all-start = ((f32[64,32,1,1,1,128]{5,1,4,3,2,0:T(8,128)}), f32[64,32,1,1,1,128]{5,1,4,3,2,0:T(8,128)S(1)}, u32[]{:S(2)}, u32[]{:S(2)}) async-start(f32[64,32,1,1,1,128]{5,1,4,3,2,0:T(8,128)} %copy.93), calls=%async_computation | async-start | bytes 2097152 | tf_op jit(solution)/shard_map/all_to_all | solution.py:30
  96.9 5.0 %sort.34 = (s32[2048]{0:T(1024)}, s32[2048]{0:T(1024)S(1)}) sort(s32[2048]{0:T(1024)S(1)} %neg.8, s32[2048]{0:T(1024)S(1)} %iota.8), dimensions={0}, to_apply=%region_0.1 | sort | flops 22528 | bytes 32768 | tf_op jit(solution)/shard_map/jit(argsort)/sort | solution.py:134
  101.9 5.0 %sort.35 = (s32[2048]{0:T(1024)}, s32[2048]{0:T(1024)S(1)}) sort(s32[2048]{0:T(1024)S(1)} %get-tuple-element.201, s32[2048]{0:T(1024)S(1)} %iota.9), dimensions={0}, to_apply=%region_6.9 | sort | flops 22528 | bytes 32768 | tf_op jit(solution)/shard_map/jit(argsort)/sort | solution.py:135
  107.0 11.8 %gather_fusion = s32[2048]{0:T(1024)S(1)} fusion(s32[2048]{0:T(1024)S(1)} %convert_element_type.20, s32[2048]{0:T(1024)S(1)} %get-tuple-element.274), kind=kCustom, calls=%fused_computation.4 | custom fusion | bytes 24576 | tf_op jit(solution)/shard_map/jit(_take)/gather | solution.py:138
  118.8 11.8 %gather_fusion.2 = f32[2048]{0:T(1024)S(1)} fusion(f32[2048]{0:T(1024)S(1)} %squeeze.14, s32[2048]{0:T(1024)S(1)} %get-tuple-element.274), kind=kCustom, calls=%fused_computation.1.clone | custom fusion | bytes 24576 | tf_op jit(solution)/shard_map/jit(_take)/gather | solution.py:137
  130.6 18.6 %all-to-all-done = f32[64,32,1,1,1,128]{5,1,4,3,2,0:T(8,128)S(1)} async-done(((f32[64,32,1,1,1,128]{5,1,4,3,2,0:T(8,128)}), f32[64,32,1,1,1,128]{5,1,4,3,2,0:T(8,128)S(1)}, u32[]{:S(2)}, u32[]{:S(2)}) %all-to-all-start) | async-done | bytes 1048608 | tf_op jit(solution)/shard_map/all_to_all | solution.py:30
  149.6 5.5 %gather_fusion.1 = f32[2048,128]{1,0:T(8,128)S(1)} fusion(f32[128,2048]{0,1:T(8,128)S(1)} %bitcast.130, s32[2048]{0:T(1024)S(1)} %get-tuple-element.274), kind=kCustom, calls=%fused_computation.clone | custom fusion | bytes 2105344 | tf_op jit(solution)/shard_map/jit(_take)/gather | solution.py:136
  155.1 1.3 select_bitcast_fusion.1
  156.4 1.0 broadcast_in_dim.65
  157.5 23.4 %while.38 = (s32[]{:T(128)}, f32[128,2048]{0,1:T(8,128)}, f32[2048]{0:T(1024)S(1)}, f32[128,2048]{0,1:T(8,128)}, s32[2048]{0:T(1024)S(1)}, /*index=5*/f32[2048]{...) while((s32[]{:T(128)}, f32[128,2048]{0,1:T(8,128)}, ...), condition=%wide.region_5.8_spmd, body=%wide.region_1.7_spmd.sunk | while | flops 135988224 | bytes 6311812 | solution.py:158
  157.6 0.7 fusion.68
  158.3 1.0 constant_dynamic-slice_fusion.2
  159.3 4.0 %while.39 = (s32[]{:T(128)}, f32[128,512]{0,1:T(8,128)S(1)}, s32[]{:T(128)}, s32[512]{0:T(512)S(1)}, f32[512]{0:T(512)S(1)}, /*index=5*/bf16[512,128]{1,0:T(8,128)(2,1)S(1)}, bf16[128,512]{1,0:T(8,128)(2,1)S(1)}, s32[]{:T(128)}) while((s32[]{:T(128)}, f32[128,512]{0,1:T(8,128)S(1)}, s32[]{:T(128)}, s32[512]{0:T(512)S(1)}, f32[512]{0:T(512)S(1)}, ...), condition=%wide.region_4.6_spmd, body=%wide.region_3.5_spmd.sunk | while | flops 135135744 | bytes 4199521 | solution.py:125
  160.3 0.7 fusion.73
  161.9 0.7 fusion.73
  163.9 0.7 constant_dynamic-update-slice_fusion.7
  164.7 0.7 fusion.68
  165.4 1.0 constant_dynamic-slice_fusion.2
  166.4 2.3 while.39
  167.4 0.7 fusion.73
  169.4 0.7 constant_dynamic-update-slice_fusion.7
  170.2 0.7 fusion.68
  170.9 1.0 constant_dynamic-slice_fusion.2
  171.9 2.3 while.39
  172.8 0.7 fusion.73
  174.8 0.7 constant_dynamic-update-slice_fusion.7
  175.6 0.7 fusion.68
  176.3 1.0 constant_dynamic-slice_fusion.2
  177.3 2.3 while.39
  178.3 0.7 fusion.73
  180.2 0.7 constant_dynamic-update-slice_fusion.7
  180.9 11.8 %gather_fusion.4 = f32[2048]{0:T(1024)S(1)} fusion(f32[2048]{0:T(1024)S(1)} %get-tuple-element.480, s32[2048]{0:T(1024)S(1)} %get-tuple-element.275), kind=kCustom, calls=%fused_computation.3.clone | custom fusion | bytes 24576 | tf_op jit(solution)/shard_map/jit(_take)/gather | solution.py:164
  192.7 5.5 %gather_fusion.3 = f32[2048,128]{1,0:T(8,128)S(1)} fusion(f32[128,2048]{0,1:T(8,128)S(1)} %copy-done.1, s32[2048]{0:T(1024)S(1)} %get-tuple-element.275), kind=kCustom, calls=%fused_computation.2.clone | custom fusion | bytes 2105344 | tf_op jit(solution)/shard_map/jit(_take)/gather | solution.py:164
  198.8 11.1 %all-to-all-start.3 = ((f32[64,1,1,1,1,128]{5,4,3,2,1,0:T(1,128)}), f32[64,1,1,1,1,128]{5,4,3,2,1,0:T(1,128)S(1)}, u32[]{:S(2)}, u32[]{:S(2)}) async-start(f32[64,1,1,1,1,128]{5,4,3,2,1,0:T(1,128)} %bitcast.45), calls=%async_computation.3 | async-start | bytes 65536 | tf_op jit(solution)/shard_map/all_to_all | solution.py:30
  210.8 1.3 copy.98
  212.1 13.5 %all-to-all-done.3 = f32[64,1,1,1,1,128]{5,4,3,2,1,0:T(1,128)S(1)} async-done(((f32[64,1,1,1,1,128]{5,4,3,2,1,0:T(1,128)}), f32[64,1,1,1,1,128]{5,4,3,2,1,0:T(1,128)S(1)}, u32[]{:S(2)}, u32[]{:S(2)}) %all-to-all-start.3) | async-done | bytes 32800 | tf_op jit(solution)/shard_map/all_to_all | solution.py:30
  225.6 5.5 %all-to-all-start.2 = ((f32[64,32,1,1,1,128]{5,1,4,3,2,0:T(8,128)}), f32[64,32,1,1,1,128]{5,1,4,3,2,0:T(8,128)}, u32[]{:S(2)}, u32[]{:S(2)}) async-start(f32[64,32,1,1,1,128]{5,1,4,3,2,0:T(8,128)} %bitcast.133), calls=%async_computation.2 | async-start | bytes 2097152 | tf_op jit(solution)/shard_map/all_to_all | solution.py:30
  231.2 1.2 fusion.20
  232.7 1.3 fusion.47
  234.1 1.3 dynamic-slice_add_fusion
  235.4 47.0 %all-to-all-done.2 = f32[64,32,1,1,1,128]{5,1,4,3,2,0:T(8,128)} async-done(((f32[64,32,1,1,1,128]{5,1,4,3,2,0:T(8,128)}), f32[64,32,1,1,1,128]{5,1,4,3,2,0:T(8,128)}, u32[]{:S(2)}, u32[]{:S(2)}) %all-to-all-start.2) | async-done | bytes 1048608 | tf_op jit(solution)/shard_map/all_to_all | solution.py:30
  282.4 2.8 copy.106
  (101 shorter events, 13.3 us)
Async XLA Ops:
  0.6 42.7 %copy-start = (f32[32,4,16,128]{3,2,1,0:T(8,128)S(1)}, f32[32,4,16,128]{3,2,1,0:T(8,128)}, u32[]{:S(2)}) copy-start(f32[32,4,16,128]{3,2,1,0:T(8,128)} %param.18) | copy-start | bytes 3145732
  14.7 28.6 %copy-start.9 = (f32[5,4,16,128]{3,2,1,0:T(8,128)}, f32[5,4,16,128]{3,2,1,0:T(8,128)S(1)}, u32[]{:S(2)}) copy-start(f32[5,4,16,128]{3,2,1,0:T(8,128)S(1)} %all_gather.3) | copy-start | bytes 491524
  16.9 57.5 %all-to-all-start.1 = ((f32[64,1,1,1,1,64]{5,4,3,2,1,0:T(1,128)}), f32[64,1,1,1,1,64]{5,4,3,2,1,0:T(1,128)S(1)}, u32[]{:S(2)}, u32[]{:S(2)}) async-start(f32[64,1,1,1,1,64]{5,4,3,2,1,0:T(1,128)} %bitcast.11), calls=%async_computation.1 | async-start | bytes 65536 | tf_op jit(solution)/shard_map/all_to_all | solution.py:30
  39.1 24.7 %collective-permute-start.1 = (f32[35,4,1,128]{3,2,1,0:T(1,128)}, f32[35,4,1,128]{3,2,1,0:T(1,128)S(1)}, u32[]{:S(2)}, u32[]{:S(2)}) collective-permute-start(f32[35,4,1,128]{3,2,1,0:T(1,128)} %get-tuple-element.257), channel_id=1, source_target_pairs={{0,8},{8,16},{16,24},{24,32},{32,40},{40,48},{48,56},{56,64},{64,7... | collective-permute-start | bytes 215048 | tf_op jit(solution)/shard_map/ppermute | solution.py:43
  42.1 21.8 %collective-permute-start.2 = (f32[35,4,1,128]{3,2,1,0:T(1,128)}, f32[35,4,1,128]{3,2,1,0:T(1,128)}, u32[]{:S(2)}, u32[]{:S(2)}) collective-permute-start(f32[35,4,1,128]{3,2,1,0:T(1,128)} %get-tuple-element.258), channel_id=1, source_target_pairs={{8,0},{16,8},{24,16},{32,24},{40,32},{48,40},{56,48},{64,56},{72,6... | collective-permute-start | bytes 215048 | tf_op jit(solution)/shard_map/ppermute | solution.py:44
  45.2 15.0 %collective-permute-start.3 = (f32[35,4,16,1]{0,2,3,1:T(8,128)}, f32[35,4,16,1]{0,2,3,1:T(8,128)S(1)}, u32[]{:S(2)}, u32[]{:S(2)}) collective-permute-start(f32[35,4,16,1]{0,2,3,1:T(8,128)} %copy.90), channel_id=1, source_target_pairs={{1,0},{2,1},{3,2},{4,3},{5,4},{6,5},{7,6},{9,8},{10,9},{11,10},{12... | collective-permute-start | bytes 26888 | tf_op jit(solution)/shard_map/ppermute | solution.py:44
  52.3 4.4 %collective-permute-start = (f32[35,4,16,1]{0,2,3,1:T(8,128)S(1)}, f32[35,4,16,1]{0,2,3,1:T(8,128)S(1)}, u32[]{:S(2)}, u32[]{:S(2)}) collective-permute-start(f32[35,4,16,1]{0,2,3,1:T(8,128)S(1)} %copy.88), channel_id=1, source_target_pairs={{0,1},{1,2},{2,3},{3,4},{4,5},{5,6},{6,7},{8,9},{9,10},{10,11},{11... | collective-permute-start | bytes 26888 | tf_op jit(solution)/shard_map/ppermute | solution.py:43
  60.2 4.7 %copy-start.4 = (f32[35,4,18,1]{3,2,1,0:T(8,128)}, f32[35,4,18,1]{3,2,1,0:T(8,128)S(1)}, u32[]{:S(2)}) copy-start(f32[35,4,18,1]{3,2,1,0:T(8,128)S(1)} %pad.9) | copy-start | bytes 30244
  63.8 1.2 copy-start.6
  71.1 1.1 copy-start.8
  74.4 74.7 %all-to-all-start = ((f32[64,32,1,1,1,128]{5,1,4,3,2,0:T(8,128)}), f32[64,32,1,1,1,128]{5,1,4,3,2,0:T(8,128)S(1)}, u32[]{:S(2)}, u32[]{:S(2)}) async-start(f32[64,32,1,1,1,128]{5,1,4,3,2,0:T(8,128)} %copy.93), calls=%async_computation | async-start | bytes 2097152 | tf_op jit(solution)/shard_map/all_to_all | solution.py:30
  155.1 2.4 copy-start.2
  155.1 2.4 copy-start.3
  155.1 2.4 copy-start.10
  180.9 11.8 %copy-start.1 = (f32[128,2048]{0,1:T(8,128)S(1)}, f32[128,2048]{0,1:T(8,128)}, u32[]{:S(2)}) copy-start(f32[128,2048]{0,1:T(8,128)} %get-tuple-element.479) | copy-start | bytes 3145732
  198.8 26.7 %all-to-all-start.3 = ((f32[64,1,1,1,1,128]{5,4,3,2,1,0:T(1,128)}), f32[64,1,1,1,1,128]{5,4,3,2,1,0:T(1,128)S(1)}, u32[]{:S(2)}, u32[]{:S(2)}) async-start(f32[64,1,1,1,1,128]{5,4,3,2,1,0:T(1,128)} %bitcast.45), calls=%async_computation.3 | async-start | bytes 65536 | tf_op jit(solution)/shard_map/all_to_all | solution.py:30
  212.1 19.1 %copy-start.5 = (f32[35,4,18,1]{3,2,1,0:T(8,128)S(1)}, f32[35,4,18,1]{3,2,1,0:T(8,128)}, u32[]{:S(2)}) copy-start(f32[35,4,18,1]{3,2,1,0:T(8,128)} %copy-done.4) | copy-start | bytes 30244
  225.6 56.8 %all-to-all-start.2 = ((f32[64,32,1,1,1,128]{5,1,4,3,2,0:T(8,128)}), f32[64,32,1,1,1,128]{5,1,4,3,2,0:T(8,128)}, u32[]{:S(2)}, u32[]{:S(2)}) async-start(f32[64,32,1,1,1,128]{5,1,4,3,2,0:T(8,128)} %bitcast.133), calls=%async_computation.2 | async-start | bytes 2097152 | tf_op jit(solution)/shard_map/all_to_all | solution.py:30
  231.2 1.6 copy-start.7
where the time goes:
time: 287 us; the launch traced here: 285 us
  local copies, waits for them, and re-layouts  79.4 us (28%)
  waiting for transfers between devices  79 us (28%)
  starting transfers between devices  72 us (25%)
  other arithmetic  32 us (11%)
  blocking collectives  10.5 us (4%)
  loops' own time  6.19 us (2%)
  matrix products  4.96 us (2%)
    all_to_all x4, waiting for transfers between devices, one_exchange(): lax.all_to_all(pieces, axis, split_axis=0, concat_axis=0, tiled=True)  79 us
    all_to_all x4, starting transfers between devices, one_exchange(): lax.all_to_all(pieces, axis, split_axis=0, concat_axis=0, tiled=True)  58.9 us
    gather x2, local copies, waits for them, and re-layouts, react_cells(): return (jnp.take(reacted, inverse, axis=1), jnp.take(heated, inverse))  17.3 us
    gather x1, local copies, waits for them, and re-layouts, react_cells(): sorted_rates = jnp.take(rate_cells, sort_order)  11.8 us
    gather x1, local copies, waits for them, and re-layouts, react_cells(): sorted_counts = jnp.take(count_cells, sort_order)  11.8 us
    all_gather x1, blocking collectives, local(): lax.all_gather(jnp.stack([zonal_cell_fraction, meridional_cell_fraction,...  10.5 us
    ppermute x2, starting transfers between devices, extended(): lax.ppermute(leading, axis, [(b, a) for a, b in up])  7.59 us
    another operation x4, loops' own time, react_block(): lax.while_loop(keep_going, substep, (jnp.zeros((), jnp.int32), tracer_blo...  6.09 us
  transfers between devices with their start and end apart: 8, of which 3 were waited for; matrix products, arithmetic and copies ran while one was open for 22% of the time, Pallas kernels for 0%

commit v1 on v0

v1 whole, which is shorter than its diff:
```python
import functools

import jax
import jax.numpy as jnp
from jax import lax
from jax.experimental import pallas as pl
from jax.experimental.pallas import tpu as pltpu
from jax.sharding import PartitionSpec as P

MESH = pl.DeviceIdType.MESH
diffusion = 0.1
pressure = 0.05
chem_step = 0.2


def kernel(
    sizes,
    species,
    east,
    north,
    up,
    warm,
    dens,
    counts,
    comp,
    stoi,
    heat,
    back,
    small,
    raw,
    cells,
    packs,
    sides,
    adv,
    block,
    reacted,
    own,
    winds,
    side_u,
    side_vt,
    rim_out,
    rim_in,
    coef,
    misc,
    count_v,
    comp_v,
    stoi_v,
    heat_v,
    heat_b,
    small_v,
    load_sem,
    wind_sem,
    lat_sem,
    rim_sem,
    lon_sem,
    lonu_sem,
    lonv_sem,
    fwd_sem,
    back_sem,
    local_sem,
    out_sem,
):
    groups, lats, lons = sizes
    g, la, lo = lax.axis_index("group"), lax.axis_index("lat"), lax.axis_index("lon")
    levels, rows, own_tr, width = adv.shape
    species_all = comp_v.shape[1]
    repeats = comp_v.shape[0] // species_all
    pieces = rows // 2
    peers = [lax.rem(g + k, groups) for k in range(1, groups)]
    has_s, has_n, has_w, has_e = la > 0, la < lats - 1, lo > 0, lo < lons - 1
    dev_s, dev_n, dev_w, dev_e = (g, la - 1, lo), (g, la + 1, lo), (g, la, lo - 1), (g, la, lo + 1)

    barrier = pltpu.get_barrier_semaphore()

    def greet(dev):
        pl.semaphore_signal(barrier, inc=1, device_id=dev, device_id_type=MESH)

    for p in peers:
        greet((p, la, lo))
    for has, dev in ((has_s, dev_s), (has_n, dev_n), (has_w, dev_w), (has_e, dev_e)):
        pl.when(has)(functools.partial(greet, dev))

    part = own_tr * levels * rows // 4
    loads = [
        pltpu.make_async_copy(src, dst, load_sem.at[i])
        for i, (src, dst) in enumerate(
            [
                (species.at[pl.ds(n * part, part)], raw.at[pl.ds(n * part, part)])
                for n in range(4)
            ]
            + [
                (up.at[0], own.at[0]),
                (east.at[0], own.at[1]),
                (north.at[0], own.at[2]),
                (warm.at[0], own.at[3]),
                (dens.at[0], misc.at[0]),
                (counts, count_v),
                (comp, comp_v),
                (stoi, stoi_v),
                (heat, heat_v),
            ]
        )
    ]
    for i in list(range(4, 8)) + list(range(4)) + list(range(8, 13)):
        loads[i].start()

    @pl.when(jnp.logical_not(has_s))
    def _():
        cells[:, 0] = jnp.zeros((levels, own_tr, width), jnp.float32)
        rim_in[0] = jnp.zeros((8, width), jnp.float32)

    @pl.when(jnp.logical_not(has_n))
    def _():
        cells[:, rows + 1] = jnp.zeros((levels, own_tr, width), jnp.float32)
        rim_in[1] = jnp.zeros((8, width), jnp.float32)

    @pl.when(jnp.logical_not(has_w))
    def _():
        sides[0] = jnp.zeros((own_tr, width), jnp.float32)
        side_u[0] = jnp.zeros((levels, rows, width), jnp.float32)
        side_vt[0] = jnp.zeros((2, rows, width), jnp.float32)

    @pl.when(jnp.logical_not(has_e))
    def _():
        sides[1] = jnp.zeros((own_tr, width), jnp.float32)
        side_u[1] = jnp.zeros((levels, rows, width), jnp.float32)
        side_vt[1] = jnp.zeros((2, rows, width), jnp.float32)

    lane = lax.broadcasted_iota(jnp.int32, (own_tr, width), 1)

    for i in range(4):
        loads[i].wait()

    def turn(r, packed):
        west, eastern = packed
        for l in range(levels):
            q = l * rows + r
            tile = raw[pl.ds(q, own_tr, stride=levels * rows), :]
            cells[l, r + 1] = tile
            hit = lane == q
            west = jnp.where(hit, pltpu.roll(tile, q, 1), west)
            eastern = jnp.where(hit, pltpu.roll(tile, q + 1, 1), eastern)
        return west, eastern

    zero = jnp.zeros((own_tr, width), jnp.float32)
    west, eastern = lax.fori_loop(0, rows, turn, (zero, zero))
    packs[0] = eastern
    packs[1] = west
    for i in range(4, 8):
        loads[i].wait()
    winds[g] = own[0:3]

    n_greet = (
        groups
        - 1
        + has_s.astype(jnp.int32)
        + has_n.astype(jnp.int32)
        + has_w.astype(jnp.int32)
        + has_e.astype(jnp.int32)
    )
    pl.semaphore_wait(barrier, n_greet)

    def remote(src, dst, sems, index, dev):
        return pltpu.make_async_remote_copy(
            src_ref=src,
            dst_ref=dst,
            send_sem=sems.at[(0,) + index],
            recv_sem=sems.at[(1,) + index],
            device_id=dev,
            device_id_type=MESH,
        )

    def wind_copy(k, level):
        return remote(own.at[pl.ds(0, 3)], winds.at[level], wind_sem, (k,), (peers[k], la, lo))

    for k in range(groups - 1):
        wind_copy(k, g).start()
    lon_copies = [
        (has_e, has_w, remote(packs.at[0], sides.at[0], lon_sem, (0,), dev_e)),
        (has_w, has_e, remote(packs.at[1], sides.at[1], lon_sem, (1,), dev_w)),
    ]
    lat_copies = [
        (has_n, has_s, remote(cells.at[:, rows], cells.at[:, 0], lat_sem, (0,), dev_n)),
        (has_s, has_n, remote(cells.at[:, 1], cells.at[:, rows + 1], lat_sem, (1,), dev_s)),
    ]
    lonv_copies = [
        (has_e, has_w, remote(own.at[pl.ds(2, 2)], side_vt.at[0], lonv_sem, (0,), dev_e)),
        (has_w, has_e, remote(own.at[pl.ds(2, 2)], side_vt.at[1], lonv_sem, (1,), dev_w)),
    ]
    wind_u = winds.at[:, 1]
    lonu_copies = [
        (has_e, has_w, remote(wind_u, side_u.at[0], lonu_sem, (0,), dev_e)),
        (has_w, has_e, remote(wind_u, side_u.at[1], lonu_sem, (1,), dev_w)),
    ]
    rim_copies = [
        (has_n, has_s, remote(rim_out.at[0], rim_in.at[0], rim_sem, (0,), dev_n)),
        (has_s, has_n, remote(rim_out.at[1], rim_in.at[1], rim_sem, (1,), dev_s)),
    ]

    def start_all(copies):
        for sends, _, copy in copies:
            pl.when(sends)(copy.start)

    def receive_all(copies):
        for _, receives, copy in copies:
            pl.when(receives)(copy.wait_recv)

    start_all(lon_copies)
    start_all(lat_copies)

    for k in range(groups - 1):
        wind_copy(k, lax.rem(g + groups - 1 - k, groups)).wait_recv()
    start_all(lonu_copies)
    for l in range(levels):
        rim_out[0, l : l + 1, :] = winds[l, 2, rows - 1 : rows, :]
        rim_out[1, l : l + 1, :] = winds[l, 2, 0:1, :]
    for j in range(3):
        rim_out[0, levels + j : levels + j + 1, :] = own[1 + j, rows - 1 : rows, :]
        rim_out[1, levels + j : levels + j + 1, :] = own[1 + j, 0:1, :]
    start_all(rim_copies)
    start_all(lonv_copies)

    row_at = lax.broadcasted_iota(jnp.int32, (rows, width), 0)
    lane_at = lax.broadcasted_iota(jnp.int32, (rows, width), 1)

    def from_west(f, edge):
        return jnp.where(lane_at == 0, pltpu.roll(edge, 1, 1), pltpu.roll(f, 1, 1))

    def from_east(f, edge):
        return jnp.where(
            lane_at == width - 1, pltpu.roll(edge, width - 1, 1), pltpu.roll(f, width - 1, 1)
        )

    def from_south(f, edge):
        return jnp.where(row_at == 0, edge, pltpu.roll(f, 1, 0))

    def from_north(f, edge):
        return jnp.where(row_at == rows - 1, edge, pltpu.roll(f, rows - 1, 0))

    def zonal_vertical():
        for l in range(levels):
            u = winds[l, 1]
            a_e = 0.5 * (u + from_east(u, side_u[1, l]))
            a_w = 0.5 * (from_west(u, side_u[0, l]) + u)
            keep = 1.0 - jnp.maximum(a_e, 0.0) + jnp.minimum(a_w, 0.0)
            coef[1, l] = -jnp.minimum(a_e, 0.0)
            coef[2, l] = jnp.maximum(a_w, 0.0)
            if l < levels - 1:
                a_u = 0.5 * (winds[l, 0] + winds[l + 1, 0])
                keep = keep - jnp.maximum(a_u, 0.0)
                coef[5, l] = -jnp.minimum(a_u, 0.0)
            if l > 0:
                a_d = 0.5 * (winds[l - 1, 0] + winds[l, 0])
                keep = keep + jnp.minimum(a_d, 0.0)
                coef[6, l] = jnp.maximum(a_d, 0.0)
            coef[7, l] = keep

    def meridional(south_rim, north_rim):
        for l in range(levels):
            v = winds[l, 2]
            a_n = 0.5 * (v + from_north(v, north_rim(l)))
            a_s = 0.5 * (from_south(v, south_rim(l)) + v)
            coef[3, l] = -jnp.minimum(a_n, 0.0)
            coef[4, l] = jnp.maximum(a_s, 0.0)
            coef[0, l] = coef[7, l] - jnp.maximum(a_n, 0.0) + jnp.minimum(a_s, 0.0)

    receive_all(lonu_copies)
    zonal_vertical()
    meridional(lambda l: winds[l, 2, 0:1, :], lambda l: winds[l, 2, 0:1, :])
    receive_all(lon_copies)

    def first_row(i):
        odd = i % 2
        half = i // 2
        middle = pieces // 2
        return 2 * (odd * (middle + half) + (1 - odd) * (middle - 1 - half))

    mine = pl.ds(pl.multiple_of(g * own_tr, own_tr), own_tr)

    def forward_copy(i, k, part):
        r0 = first_row(i)
        part = pl.ds(pl.multiple_of(part * own_tr, own_tr), own_tr)
        return remote(
            adv.at[peers[k], pl.ds(r0, 2)],
            block.at[pl.ds(r0, 2), part],
            fwd_sem,
            (i, k),
            (peers[k], la, lo),
        )

    def advect(i, carry):
        r0 = first_row(i)
        for rr in range(2):
            r = r0 + rr
            for l in range(levels):
                q = l * rows + r

                def c(j):
                    return coef[j, l, pl.ds(r, 1), :]

                here = cells[l, r + 1]
                east_of = jnp.where(
                    lane == width - 1,
                    pltpu.roll(sides[1], width - 1 - q, 1),
                    pltpu.roll(here, width - 1, 1),
                )
                west_of = jnp.where(
                    lane == 0,
                    pltpu.roll(sides[0], lax.rem(width - q, width), 1),
                    pltpu.roll(here, 1, 1),
                )
                total = c(0) * here + c(1) * east_of + c(2) * west_of
                total = total + c(3) * cells[l, r + 2] + c(4) * cells[l, r]
                if l < levels - 1:
                    total = total + c(5) * cells[l + 1, r + 1]
                if l > 0:
                    total = total + c(6) * cells[l - 1, r + 1]
                adv[l, r] = total
            block[r, mine, :] = adv[g, r]
        for k in range(groups - 1):
            forward_copy(i, k, g).start()
        return carry

    lax.fori_loop(0, pieces - 2, advect, 0)

    receive_all(rim_copies)
    receive_all(lat_copies)
    meridional(lambda l: rim_in[0, l : l + 1, :], lambda l: rim_in[1, l : l + 1, :])
    lax.fori_loop(pieces - 2, pieces, advect, 0)

    for i in range(8, 13):
        loads[i].wait()
    receive_all(lonv_copies)
    t = own[3]
    misc[1] = 1.0 / (1.0 + jnp.exp(-2.0 * t))
    heat_b[...] = jnp.transpose(jnp.broadcast_to(heat_v[...], (species_all, species_all)))

    def around(f, j, west_tile, east_tile):
        s, n = rim_in[0, levels + j : levels + j + 1, :], rim_in[1, levels + j : levels + j + 1, :]
        return from_east(f, east_tile), from_west(f, west_tile), from_north(f, n), from_south(f, s)

    t_e, t_w, t_n, t_s = around(t, 2, side_vt[0, 1], side_vt[1, 1])
    u = own[1]
    e, w, n, s = around(u, 0, side_u[0, g], side_u[1, g])
    small_v[0] = u + diffusion * (e + w + n + s - 4.0 * u) - pressure * (t_e - t_w)
    v = own[2]
    e, w, n, s = around(v, 1, side_vt[0, 0], side_vt[1, 0])
    small_v[1] = v + diffusion * (e + w + n + s - 4.0 * v) - pressure * (t_n - t_s)
    misc[2] = t + diffusion * (t_e + t_w + t_n + t_s - 4.0 * t)

    def back_copy(i, k, level):
        r0 = first_row(i)
        part = pl.ds(pl.multiple_of(peers[k] * own_tr, own_tr), own_tr)
        return remote(
            reacted.at[pl.ds(r0, 2), part],
            back.at[level, pl.ds(r0, 2)],
            back_sem,
            (i, k),
            (peers[k], la, lo),
        )

    def local_copy(i):
        r0 = first_row(i)
        return pltpu.make_async_copy(
            reacted.at[pl.ds(r0, 2), mine], back.at[g, pl.ds(r0, 2)], local_sem.at[i]
        )

    twice = (la + 1) * rows > 3 * lats * rows // 4

    def react(i, carry):
        r0 = first_row(i)
        for k in range(groups - 1):
            forward_copy(i, k, lax.rem(g + groups - 1 - k, groups)).wait_recv()

        def pair_of(ref):
            return jnp.concatenate([ref[pl.ds(r0, 1), :], ref[pl.ds(r0 + 1, 1), :]], axis=1)

        rate = pair_of(misc.at[1])
        count = pair_of(count_v)

        def substep(current, counter):
            narrow = current.astype(jnp.bfloat16)
            pair_terms = jnp.dot(comp_v[...], narrow, preferred_element_type=jnp.float32)
            quad = (
                (pair_terms.reshape(repeats, species_all, 2 * width) * current[None])
                .reshape(repeats * species_all, 2 * width)
                .astype(jnp.bfloat16)
            )
            made = jnp.dot(stoi_v[...], quad, preferred_element_type=jnp.float32)
            later = current + chem_step * (rate * made - current)
            return jnp.where(counter < count, later, current)

        def load(ref):
            return jnp.concatenate([ref[r0], ref[r0 + 1]], axis=1)

        def keep(value):
            reacted[r0] = value[:, :width]
            reacted[r0 + 1] = value[:, width:]

        keep(substep(load(block), 0))

        @pl.when(twice)
        def _():
            keep(substep(load(reacted), 1))

        for k in range(groups - 1):
            back_copy(i, k, g).start()
        local_copy(i).start()
        for rr in range(2):
            r = r0 + rr
            gain = heat_b[...] * (reacted[r] - block[r])
            misc[3, pl.ds(r, 1), :] = jnp.sum(gain, axis=0, keepdims=True)
        return carry

    lax.fori_loop(0, pieces, react, 0)

    small_v[2] = misc[2] + misc[3] / misc[0]
    out = pltpu.make_async_copy(small_v, small, out_sem)
    out.start()

    for sends, _, copy in lon_copies + lat_copies + lonv_copies + lonu_copies + rim_copies:
        pl.when(sends)(copy.wait_send)
    for k in range(groups - 1):
        wind_copy(k, g).wait_send()

    def finish(i, carry):
        for k in range(groups - 1):
            forward_copy(i, k, g).wait_send()
            back_copy(i, k, g).wait_send()
            back_copy(i, k, lax.rem(g + groups - 1 - k, groups)).wait_recv()
        local_copy(i).wait()
        return carry

    lax.fori_loop(0, pieces, finish, 0)
    out.wait()


def unload(back, small, tracers, east, north, temp):
    levels, rows, some, width = back.shape
    for t in range(some):
        for l in range(levels):
            for r in range(0, rows, 8):
                tracers[t, l, r : r + 8, :] = back[l, r : r + 8, t, :]

    @pl.when(pl.program_id(0) == 0)
    def _():
        east[0] = small[0]
        north[0] = small[1]
        temp[0] = small[2]


def local(sizes, species, east, north, up, warm, dens, counts, comp, stoi, heat):
    own_tr, levels, rows, width = species.shape
    all_tr, terms = stoi.shape
    groups = sizes[0]
    pieces = rows // 2
    f32 = jnp.float32
    dma = pltpu.SemaphoreType.DMA
    back, small = pl.pallas_call(
        functools.partial(kernel, sizes),
        out_shape=(
            jax.ShapeDtypeStruct((levels, rows, own_tr, width), f32),
            jax.ShapeDtypeStruct((3, rows, width), f32),
        ),
        in_specs=[pl.BlockSpec(memory_space=pltpu.HBM)] * 10,
        out_specs=[pl.BlockSpec(memory_space=pltpu.HBM)] * 2,
        scratch_shapes=[
            pltpu.VMEM((own_tr * levels * rows, width), f32),
            pltpu.VMEM((levels, rows + 2, own_tr, width), f32),
            pltpu.VMEM((2, own_tr, width), f32),
            pltpu.VMEM((2, own_tr, width), f32),
            pltpu.VMEM((levels, rows, own_tr, width), f32),
            pltpu.VMEM((rows, all_tr, width), f32),
            pltpu.VMEM((rows, all_tr, width), f32),
            pltpu.VMEM((4, rows, width), f32),
            pltpu.VMEM((levels, 3, rows, width), f32),
            pltpu.VMEM((2, levels, rows, width), f32),
            pltpu.VMEM((2, 2, rows, width), f32),
            pltpu.VMEM((2, 8, width), f32),
            pltpu.VMEM((2, 8, width), f32),
            pltpu.VMEM((8, levels, rows, width), f32),
            pltpu.VMEM((4, rows, width), f32),
            pltpu.VMEM((rows, width), jnp.int32),
            pltpu.VMEM((terms, all_tr), jnp.bfloat16),
            pltpu.VMEM((all_tr, terms), jnp.bfloat16),
            pltpu.VMEM((1, all_tr), f32),
            pltpu.VMEM((all_tr, all_tr), f32),
            pltpu.VMEM((3, rows, width), f32),
            dma((13,)),
            dma((2, groups - 1)),
            dma((2, 2)),
            dma((2, 2)),
            dma((2, 2)),
            dma((2, 2)),
            dma((2, 2)),
            dma((2, pieces, groups - 1)),
            dma((2, pieces, groups - 1)),
            dma((pieces,)),
            dma(()),
        ],
        compiler_params=pltpu.CompilerParams(
            collective_id=0, has_side_effects=True, vmem_limit_bytes=63 << 20
        ),
        name="couple",
    )(
        species.reshape(own_tr * levels * rows, width),
        east,
        north,
        up,
        warm,
        dens,
        counts,
        comp,
        stoi,
        heat.reshape(1, all_tr),
    )
    some = 8
    field = pl.BlockSpec((1, rows, width), lambda i: (0, 0, 0))
    return pl.pallas_call(
        unload,
        grid=(own_tr // some,),
        out_shape=(jax.ShapeDtypeStruct((own_tr, levels, rows, width), f32),)
        + (jax.ShapeDtypeStruct((1, rows, width), f32),) * 3,
        in_specs=[
            pl.BlockSpec((levels, rows, some, width), lambda i: (0, 0, i, 0)),
            pl.BlockSpec((3, rows, width), lambda i: (0, 0, 0)),
        ],
        out_specs=[
            pl.BlockSpec((some, levels, rows, width), lambda i: (i, 0, 0, 0)),
            field,
            field,
            field,
        ],
        name="unload",
    )(back, small)


def solution(mesh):
    sizes = (mesh.shape["group"], mesh.shape["lat"], mesh.shape["lon"])
    fields = P("group", "lat", "lon")
    return jax.shard_map(
        functools.partial(local, sizes),
        mesh=mesh,
        in_specs=(
            P("group", None, "lat", "lon"),
            fields,
            fields,
            fields,
            fields,
            fields,
            P("lat", "lon"),
            P(),
            P(),
            P(),
        ),
        out_specs=(P("group", None, "lat", "lon"), fields, fields, fields),
        check_vma=False,
    )
```

time: 287 us -> 46 us (0.16)
  local copies, waits for them, and re-layouts: 79.4 us -> 0 us
  waiting for transfers between devices: 79 us -> 0 us
  starting transfers between devices: 72 us -> 0 us
  Pallas kernels: 0 us -> 45 us
  other arithmetic: 32 us -> 0 us
  blocking collectives: 10.5 us -> 0 us
  loops' own time: 6.19 us -> 0 us
  matrix products: 4.96 us -> 0 us
    all_to_all x4 -> x0, waiting for transfers between devices: 79 us -> none  [one_exchange(): lax.all_to_all(pieces, axis, split_axis=0, concat_axis=0, tiled=True)]
    all_to_all x4 -> x0, starting transfers between devices: 58.9 us -> none  [one_exchange(): lax.all_to_all(pieces, axis, split_axis=0, concat_axis=0, tiled=True)]
    gather x5 -> x0, local copies, waits for them, and re-layouts: 46.3 us -> none  [the longest x2 17.3 us: react_cells(): return (jnp.take(reacted, inverse, axis=1), jnp.take(heated, inverse))]
    pallas_call x0 -> x2, Pallas kernels: none -> 45 us  [the longest x1 41.4 us: local(): pl.pallas_call(functools.partial(kernel, sizes), out_shape=(jax.ShapeDtyp...]
    ppermute x4 -> x0, starting transfers between devices: 13 us -> none  [the longest x2 7.59 us: extended(): lax.ppermute(leading, axis, [(b, a) for a, b in up])]
    all_gather x1 -> x0, blocking collectives: 10.5 us -> none  [local(): lax.all_gather(jnp.stack([zonal_cell_fraction, meridional_cell_fraction,...]
    sort x2 -> x0, other arithmetic: 10.1 us -> none  [the longest x1 5.04 us: react_cells(): sort_order = jnp.argsort(-count_cells, stable=True)]
    another operation x5 -> x0, loops' own time: 6.19 us -> none  [the longest x4 6.09 us: react_block(): lax.while_loop(keep_going, substep, (jnp.zeros((), jnp.int32), tracer_blo...]
  transfers between devices with their start and end apart: 8 -> 0, of which waited for: 3 -> 0; matrix products, arithmetic and copies ran while one was open for 22% -> 0% of each run, Pallas kernels for 0% -> 0%
where the time goes in v1:
time: 46 us; the launch traced here: 45.7 us
  Pallas kernels  45 us (98%)
  between operations  0.64 us (1%)
    pallas_call x1, Pallas kernels, local(): pl.pallas_call(functools.partial(kernel, sizes), out_shape=(jax.ShapeDtyp...  41.4 us
    pallas_call x1, Pallas kernels, local(): pl.pallas_call(unload, grid=(own_tr // some,), out_shape=(jax.ShapeDtypeS...  3.62 us

profile of v1, /device:TPU:1, one launch (start us, length us, event | category | flops | bytes accessed | tf_op | source)
XLA Modules:
  0.0 45.7 jit_solution(9719478555753083450)
XLA Ops:
  0.6 41.4 %couple.1 = (f32[4,16,32,128]{3,2,1,0:T(8,128)}, f32[3,16,128]{2,1,0:T(8,128)}) custom-call(f32[2048,128]{1,0:T(8,128)} %bitcast.2, f32[1,16,128]{2,1,0:T(8,128)} %east.1, f32[1,16,128]{2,1,0:T(8,128)} %north.1, f32[1,16,128]{2,1,0:T(8,128)} %up.1, f32[1,16,128]{2,1,0:T(8,128)} %warm.1, f32[1,16,128]{2,1,0:T(8,128)} %dens.1, s32[16,128]{1,0:T(8,128)} %counts.1, ...), custom_call_target="tpu_custom_call" | custom-call | tf_op jit(solution)/shard_map/couple/pallas_call | solution.py:459
  42.0 3.6 %unload.1 = (f32[32,4,16,128]{3,2,1,0:T(8,128)}, f32[1,16,128]{2,1,0:T(8,128)}, f32[1,16,128]{2,1,0:T(8,128)}, f32[1,16,128]{2,1,0:T(8,128)}) custom-call(f32[4,16,32,128]{3,2,1,0:T(8,128)} %get-tuple-element.6.back, f32[3,16,128]{2,1,0:T(8,128)} %get-tuple-element.7.small), custom_call_target="tpu_custom_call" | custom-call | tf_op jit(solution)/shard_map/unload/pallas_call | solution.py:519

commit v2 on v1

--- a/solution.py
+++ b/solution.py
@@ -25,8 +25,10 @@
     comp,
     stoi,
     heat,
-    back,
-    small,
+    tracers,
+    east_out,
+    north_out,
+    temp_out,
     raw,
     cells,
     packs,
@@ -34,6 +36,7 @@
     adv,
     block,
     reacted,
+    back,
     own,
     winds,
     side_u,
@@ -47,7 +50,6 @@
     stoi_v,
     heat_v,
     heat_b,
-    small_v,
     load_sem,
     wind_sem,
     lat_sem,
@@ -57,8 +59,7 @@
     lonv_sem,
     fwd_sem,
     back_sem,
-    local_sem,
-    out_sem,
+    ok_sem,
 ):
     groups, lats, lons = sizes
     g, la, lo = lax.axis_index("group"), lax.axis_index("lat"), lax.axis_index("lon")
@@ -70,6 +71,16 @@
     has_s, has_n, has_w, has_e = la > 0, la < lats - 1, lo > 0, lo < lons - 1
     dev_s, dev_n, dev_w, dev_e = (g, la - 1, lo), (g, la + 1, lo), (g, la, lo - 1), (g, la, lo + 1)
 
+    turned = la == 3 * lats // 4
+    odd = lax.rem(lo, 2) == 1
+    near = [
+        (has_s, dev_s, turned),
+        (has_n, dev_n, la != 3 * lats // 4 - 1),
+        (has_w, dev_w, odd),
+        (has_e, dev_e, odd),
+    ]
+    leads = [jnp.logical_and(has, lead) for has, _, lead in near]
+    follows = [jnp.logical_and(has, jnp.logical_not(lead)) for has, _, lead in near]
     barrier = pltpu.get_barrier_semaphore()
 
     def greet(dev):
@@ -77,8 +88,16 @@
 
     for p in peers:
         greet((p, la, lo))
-    for has, dev in ((has_s, dev_s), (has_n, dev_n), (has_w, dev_w), (has_e, dev_e)):
-        pl.when(has)(functools.partial(greet, dev))
+    for lead, (_, dev, _) in zip(leads, near):
+        pl.when(lead)(functools.partial(greet, dev))
+
+    def answer(i):
+        pl.semaphore_signal(
+            ok_sem.at[i ^ 1], inc=1, device_id=near[i][1], device_id_type=MESH
+        )
+
+    def await_answer(i):
+        pl.when(leads[i])(lambda: pl.semaphore_wait(ok_sem.at[i], 1))
 
     part = own_tr * levels * rows // 4
     loads = [
@@ -126,6 +145,30 @@
         side_u[1] = jnp.zeros((levels, rows, width), jnp.float32)
         side_vt[1] = jnp.zeros((2, rows, width), jnp.float32)
 
+    for i in range(4, 8):
+        loads[i].wait()
+    winds[g] = own[0:3]
+
+    pl.semaphore_wait(barrier, groups - 1 + sum(f.astype(jnp.int32) for f in follows))
+    for i in range(4):
+        pl.when(follows[i])(functools.partial(answer, i))
+
+    def remote(src, dst, sems, index, dev):
+        return pltpu.make_async_remote_copy(
+            src_ref=src,
+            dst_ref=dst,
+            send_sem=sems.at[(0,) + index],
+            recv_sem=sems.at[(1,) + index],
+            device_id=dev,
+            device_id_type=MESH,
+        )
+
+    def wind_copy(k, level):
+        return remote(own.at[pl.ds(0, 3)], winds.at[level], wind_sem, (k,), (peers[k], la, lo))
+
+    for k in range(groups - 1):
+        wind_copy(k, g).start()
+
     lane = lax.broadcasted_iota(jnp.int32, (own_tr, width), 1)
 
     for i in range(4):
@@ -146,35 +189,6 @@
     west, eastern = lax.fori_loop(0, rows, turn, (zero, zero))
     packs[0] = eastern
     packs[1] = west
-    for i in range(4, 8):
-        loads[i].wait()
-    winds[g] = own[0:3]
-
-    n_greet = (
-        groups
-        - 1
-        + has_s.astype(jnp.int32)
-        + has_n.astype(jnp.int32)
-        + has_w.astype(jnp.int32)
-        + has_e.astype(jnp.int32)
-    )
-    pl.semaphore_wait(barrier, n_greet)
-
-    def remote(src, dst, sems, index, dev):
-        return pltpu.make_async_remote_copy(
-            src_ref=src,
-            dst_ref=dst,
-            send_sem=sems.at[(0,) + index],
-            recv_sem=sems.at[(1,) + index],
-            device_id=dev,
-            device_id_type=MESH,
-        )
-
-    def wind_copy(k, level):
-        return remote(own.at[pl.ds(0, 3)], winds.at[level], wind_sem, (k,), (peers[k], la, lo))
-
-    for k in range(groups - 1):
-        wind_copy(k, g).start()
     lon_copies = [
         (has_e, has_w, remote(packs.at[0], sides.at[0], lon_sem, (0,), dev_e)),
         (has_w, has_e, remote(packs.at[1], sides.at[1], lon_sem, (1,), dev_w)),
@@ -205,8 +219,15 @@
         for _, receives, copy in copies:
             pl.when(receives)(copy.wait_recv)
 
-    start_all(lon_copies)
-    start_all(lat_copies)
+    def start_lat(copies, which):
+        pl.when(which[1])(copies[0][2].start)
+        pl.when(which[0])(copies[1][2].start)
+
+    start_lat(lat_copies, follows)
+    await_answer(3)
+    pl.when(has_e)(lon_copies[0][2].start)
+    await_answer(2)
+    pl.when(has_w)(lon_copies[1][2].start)
 
     for k in range(groups - 1):
         wind_copy(k, lax.rem(g + groups - 1 - k, groups)).wait_recv()
@@ -217,7 +238,7 @@
     for j in range(3):
         rim_out[0, levels + j : levels + j + 1, :] = own[1 + j, rows - 1 : rows, :]
         rim_out[1, levels + j : levels + j + 1, :] = own[1 + j, 0:1, :]
-    start_all(rim_copies)
+    start_lat(rim_copies, follows)
     start_all(lonv_copies)
 
     row_at = lax.broadcasted_iota(jnp.int32, (rows, width), 0)
@@ -323,30 +344,15 @@
 
     lax.fori_loop(0, pieces - 2, advect, 0)
 
-    receive_all(rim_copies)
-    receive_all(lat_copies)
-    meridional(lambda l: rim_in[0, l : l + 1, :], lambda l: rim_in[1, l : l + 1, :])
-    lax.fori_loop(pieces - 2, pieces, advect, 0)
-
+    await_answer(0)
+    await_answer(1)
+    start_lat(lat_copies, leads)
+    start_lat(rim_copies, leads)
     for i in range(8, 13):
         loads[i].wait()
-    receive_all(lonv_copies)
     t = own[3]
     misc[1] = 1.0 / (1.0 + jnp.exp(-2.0 * t))
     heat_b[...] = jnp.transpose(jnp.broadcast_to(heat_v[...], (species_all, species_all)))
-
-    def around(f, j, west_tile, east_tile):
-        s, n = rim_in[0, levels + j : levels + j + 1, :], rim_in[1, levels + j : levels + j + 1, :]
-        return from_east(f, east_tile), from_west(f, west_tile), from_north(f, n), from_south(f, s)
-
-    t_e, t_w, t_n, t_s = around(t, 2, side_vt[0, 1], side_vt[1, 1])
-    u = own[1]
-    e, w, n, s = around(u, 0, side_u[0, g], side_u[1, g])
-    small_v[0] = u + diffusion * (e + w + n + s - 4.0 * u) - pressure * (t_e - t_w)
-    v = own[2]
-    e, w, n, s = around(v, 1, side_vt[0, 0], side_vt[1, 0])
-    small_v[1] = v + diffusion * (e + w + n + s - 4.0 * v) - pressure * (t_n - t_s)
-    misc[2] = t + diffusion * (t_e + t_w + t_n + t_s - 4.0 * t)
 
     def back_copy(i, k, level):
         r0 = first_row(i)
@@ -357,12 +363,6 @@
             back_sem,
             (i, k),
             (peers[k], la, lo),
-        )
-
-    def local_copy(i):
-        r0 = first_row(i)
-        return pltpu.make_async_copy(
-            reacted.at[pl.ds(r0, 2), mine], back.at[g, pl.ds(r0, 2)], local_sem.at[i]
         )
 
     twice = (la + 1) * rows > 3 * lats * rows // 4
@@ -405,18 +405,50 @@
 
         for k in range(groups - 1):
             back_copy(i, k, g).start()
-        local_copy(i).start()
         for rr in range(2):
             r = r0 + rr
             gain = heat_b[...] * (reacted[r] - block[r])
             misc[3, pl.ds(r, 1), :] = jnp.sum(gain, axis=0, keepdims=True)
         return carry
 
-    lax.fori_loop(0, pieces, react, 0)
-
-    small_v[2] = misc[2] + misc[3] / misc[0]
-    out = pltpu.make_async_copy(small_v, small, out_sem)
-    out.start()
+    lax.fori_loop(0, pieces // 2, react, 0)
+
+    receive_all(rim_copies)
+    receive_all(lat_copies)
+    meridional(lambda l: rim_in[0, l : l + 1, :], lambda l: rim_in[1, l : l + 1, :])
+    lax.fori_loop(pieces - 2, pieces, advect, 0)
+
+    lax.fori_loop(pieces // 2, pieces, react, 0)
+
+    receive_all(lonv_copies)
+
+    def around(f, j, west_tile, east_tile):
+        s, n = rim_in[0, levels + j : levels + j + 1, :], rim_in[1, levels + j : levels + j + 1, :]
+        return from_east(f, east_tile), from_west(f, west_tile), from_north(f, n), from_south(f, s)
+
+    t_e, t_w, t_n, t_s = around(t, 2, side_vt[0, 1], side_vt[1, 1])
+    u = own[1]
+    e, w, n, s = around(u, 0, side_u[0, g], side_u[1, g])
+    east_out[0] = u + diffusion * (e + w + n + s - 4.0 * u) - pressure * (t_e - t_w)
+    v = own[2]
+    e, w, n, s = around(v, 1, side_vt[0, 0], side_vt[1, 0])
+    north_out[0] = v + diffusion * (e + w + n + s - 4.0 * v) - pressure * (t_n - t_s)
+    misc[2] = t + diffusion * (t_e + t_w + t_n + t_s - 4.0 * t)
+
+    temp_out[0] = misc[2] + misc[3] / misc[0]
+
+    def collect(i, carry):
+        r0 = first_row(i)
+        for k in range(groups - 1):
+            back_copy(i, k, lax.rem(g + groups - 1 - k, groups)).wait_recv()
+        for rr in range(2):
+            back[g, r0 + rr] = reacted[r0 + rr, mine, :]
+            for l in range(levels):
+                at = l * rows + r0 + rr
+                tracers[pl.ds(at, own_tr, stride=levels * rows), :] = back[l, r0 + rr]
+        return carry
+
+    lax.fori_loop(0, pieces, collect, 0)
 
     for sends, _, copy in lon_copies + lat_copies + lonv_copies + lonu_copies + rim_copies:
         pl.when(sends)(copy.wait_send)
@@ -427,26 +459,21 @@
         for k in range(groups - 1):
             forward_copy(i, k, g).wait_send()
             back_copy(i, k, g).wait_send()
-            back_copy(i, k, lax.rem(g + groups - 1 - k, groups)).wait_recv()
-        local_copy(i).wait()
         return carry
 
     lax.fori_loop(0, pieces, finish, 0)
-    out.wait()
-
-
-def unload(back, small, tracers, east, north, temp):
-    levels, rows, some, width = back.shape
-    for t in range(some):
-        for l in range(levels):
-            for r in range(0, rows, 8):
-                tracers[t, l, r : r + 8, :] = back[l, r : r + 8, t, :]
-
-    @pl.when(pl.program_id(0) == 0)
-    def _():
-        east[0] = small[0]
-        north[0] = small[1]
-        temp[0] = small[2]
+
+
+def store(tracers, east, north, temp, tracers_out, east_out, north_out, temp_out, sem):
+    parts = sem.shape[0] - 3
+    part = tracers.shape[0] // parts
+    pairs = [(tracers.at[pl.ds(n * part, part)], tracers_out.at[pl.ds(n * part, part)]) for n in range(parts)]
+    pairs += [(east, east_out), (north, north_out), (temp, temp_out)]
+    copies = [pltpu.make_async_copy(src, dst, sem.at[i]) for i, (src, dst) in enumerate(pairs)]
+    for copy in copies:
+        copy.start()
+    for copy in copies:
+        copy.wait()
 
 
 def local(sizes, species, east, north, up, warm, dens, counts, comp, stoi, heat):
@@ -456,14 +483,24 @@
     pieces = rows // 2
     f32 = jnp.float32
     dma = pltpu.SemaphoreType.DMA
-    back, small = pl.pallas_call(
+    inputs = (
+        species.reshape(own_tr * levels * rows, width),
+        east,
+        north,
+        up,
+        warm,
+        dens,
+        counts,
+        comp,
+        stoi,
+        heat.reshape(1, all_tr),
+    )
+    tracers, east, north, temp = pl.pallas_call(
         functools.partial(kernel, sizes),
-        out_shape=(
-            jax.ShapeDtypeStruct((levels, rows, own_tr, width), f32),
-            jax.ShapeDtypeStruct((3, rows, width), f32),
-        ),
+        out_shape=(pltpu.VMEM((own_tr * levels * rows, width), f32),)
+        + (pltpu.VMEM((1, rows, width), f32),) * 3,
         in_specs=[pl.BlockSpec(memory_space=pltpu.HBM)] * 10,
-        out_specs=[pl.BlockSpec(memory_space=pltpu.HBM)] * 2,
+        out_specs=[pl.BlockSpec(memory_space=pltpu.VMEM)] * 4,
         scratch_shapes=[
             pltpu.VMEM((own_tr * levels * rows, width), f32),
             pltpu.VMEM((levels, rows + 2, own_tr, width), f32),
@@ -472,6 +509,7 @@
             pltpu.VMEM((levels, rows, own_tr, width), f32),
             pltpu.VMEM((rows, all_tr, width), f32),
             pltpu.VMEM((rows, all_tr, width), f32),
+            pltpu.VMEM((levels, rows, own_tr, width), f32),
             pltpu.VMEM((4, rows, width), f32),
             pltpu.VMEM((levels, 3, rows, width), f32),
             pltpu.VMEM((2, levels, rows, width), f32),
@@ -485,7 +523,6 @@
             pltpu.VMEM((all_tr, terms), jnp.bfloat16),
             pltpu.VMEM((1, all_tr), f32),
             pltpu.VMEM((all_tr, all_tr), f32),
-            pltpu.VMEM((3, rows, width), f32),
             dma((13,)),
             dma((2, groups - 1)),
             dma((2, 2)),
@@ -495,44 +532,25 @@
             dma((2, 2)),
             dma((2, pieces, groups - 1)),
             dma((2, pieces, groups - 1)),
-            dma((pieces,)),
-            dma(()),
+            pltpu.SemaphoreType.REGULAR((4,)),
         ],
         compiler_params=pltpu.CompilerParams(
-            collective_id=0, has_side_effects=True, vmem_limit_bytes=63 << 20
+            collective_id=0, has_side_effects=True, vmem_limit_bytes=40 << 20
         ),
         name="couple",
-    )(
-        species.reshape(own_tr * levels * rows, width),
-        east,
-        north,
-        up,
-        warm,
-        dens,
-        counts,
-        comp,
-        stoi,
-        heat.reshape(1, all_tr),
-    )
-    some = 8
-    field = pl.BlockSpec((1, rows, width), lambda i: (0, 0, 0))
-    return pl.pallas_call(
-        unload,
-        grid=(own_tr // some,),
-        out_shape=(jax.ShapeDtypeStruct((own_tr, levels, rows, width), f32),)
-        + (jax.ShapeDtypeStruct((1, rows, width), f32),) * 3,
-        in_specs=[
-            pl.BlockSpec((levels, rows, some, width), lambda i: (0, 0, i, 0)),
-            pl.BlockSpec((3, rows, width), lambda i: (0, 0, 0)),
-        ],
-        out_specs=[
-            pl.BlockSpec((some, levels, rows, width), lambda i: (i, 0, 0, 0)),
-            field,
-            field,
-            field,
-        ],
-        name="unload",
-    )(back, small)
+    )(*(pltpu.with_memory_space_constraint(x, pltpu.HBM) for x in inputs))
+    parts = 4
+    results = (tracers, east, north, temp)
+    tracers, east, north, temp = pl.pallas_call(
+        store,
+        out_shape=tuple(jax.ShapeDtypeStruct(x.shape, f32) for x in results),
+        in_specs=[pl.BlockSpec(memory_space=pltpu.VMEM)] * 4,
+        out_specs=[pl.BlockSpec(memory_space=pl.ANY)] * 4,
+        scratch_shapes=[dma((parts + 3,))],
+        compiler_params=pltpu.CompilerParams(vmem_limit_bytes=40 << 20),
+        name="store",
+    )(*(pltpu.with_memory_space_constraint(x, pltpu.VMEM) for x in results))
+    return tracers.reshape(own_tr, levels, rows, width), east, north, temp
 
 
 def solution(mesh):

time: 46 us -> 41.3 us (0.90)
  Pallas kernels: 45 us -> 40.5 us
    pallas_call x2, Pallas kernels: 45 us -> 40.5 us  [the longest x1 39.5 us: local(): pl.pallas_call(functools.partial(kernel, sizes), out_shape=(pltpu.VMEM((o...]
where the time goes in v2:
time: 41.3 us; the launch traced here: 41.2 us
  Pallas kernels  40.5 us (98%)
  between operations  0.64 us (2%)
    pallas_call x1, Pallas kernels, local(): pl.pallas_call(functools.partial(kernel, sizes), out_shape=(pltpu.VMEM((o...  39.5 us
    pallas_call x1, Pallas kernels, local(): pl.pallas_call(store, out_shape=tuple((jax.ShapeDtypeStruct(x.shape, f32)...  1.03 us

profile of v2, /device:TPU:1, one launch (start us, length us, event | category | flops | bytes accessed | tf_op | source)
XLA Modules:
  0.0 41.2 jit_solution(7994644138619709181)
XLA Ops:
  0.6 39.5 %couple.1 = (f32[2048,128]{1,0:T(8,128)S(1)}, f32[1,16,128]{2,1,0:T(8,128)S(1)}, f32[1,16,128]{2,1,0:T(8,128)S(1)}, f32[1,16,128]{2,1,0:T(8,128)S(1)}) custom-call(f32[2048,128]{1,0:T(8,128)} %bitcast.3, f32[1,16,128]{2,1,0:T(8,128)} %east.1, f32[1,16,128]{2,1,0:T(8,128)} %north.1, f32[1,16,128]{2,1,0:T(8,128)} %up.1, f32[1,16,128]{2,1,0:T(8,128)} %warm.1, ...), custom_call_target="tpu_custom_call" | custom-call | tf_op jit(solution)/shard_map/couple/pallas_call | solution.py:498
  40.1 1.0 %store.1 = (f32[2048,128]{1,0:T(8,128)}, f32[1,16,128]{2,1,0:T(8,128)}, f32[1,16,128]{2,1,0:T(8,128)}, f32[1,16,128]{2,1,0:T(8,128)}) custom-call(f32[2048,128]{1,0:T(8,128)S(1)} %get-tuple-element.12.tracers, f32[1,16,128]{2,1,0:T(8,128)S(1)} %get-tuple-element.13.east, f32[1,16,128]{2,1,0:T(8,128)S(1)} %get-tuple-element.14.north, ...), custom_call_target="tpu_custom_call" | custom-call | tf_op jit(solution)/shard_map/store/pallas_call | solution.py:544

commit v3 on v2

--- a/solution.py
+++ b/solution.py
@@ -32,15 +32,16 @@
     raw,
     cells,
     packs,
-    sides,
+    edges,
+    edges_in,
+    fix,
     adv,
     block,
     reacted,
     back,
     own,
     winds,
-    side_u,
-    side_vt,
+    side_in,
     rim_out,
     rim_in,
     coef,
@@ -54,9 +55,9 @@
     wind_sem,
     lat_sem,
     rim_sem,
+    pack_sem,
     lon_sem,
-    lonu_sem,
-    lonv_sem,
+    side_sem,
     fwd_sem,
     back_sem,
     ok_sem,
@@ -135,19 +136,13 @@
 
     @pl.when(jnp.logical_not(has_w))
     def _():
-        sides[0] = jnp.zeros((own_tr, width), jnp.float32)
-        side_u[0] = jnp.zeros((levels, rows, width), jnp.float32)
-        side_vt[0] = jnp.zeros((2, rows, width), jnp.float32)
+        edges_in[0] = jnp.zeros((species_all, width), jnp.float32)
+        side_in[0] = jnp.zeros((3, rows, width), jnp.float32)
 
     @pl.when(jnp.logical_not(has_e))
     def _():
-        sides[1] = jnp.zeros((own_tr, width), jnp.float32)
-        side_u[1] = jnp.zeros((levels, rows, width), jnp.float32)
-        side_vt[1] = jnp.zeros((2, rows, width), jnp.float32)
-
-    for i in range(4, 8):
-        loads[i].wait()
-    winds[g] = own[0:3]
+        edges_in[1] = jnp.zeros((species_all, width), jnp.float32)
+        side_in[1] = jnp.zeros((3, rows, width), jnp.float32)
 
     pl.semaphore_wait(barrier, groups - 1 + sum(f.astype(jnp.int32) for f in follows))
     for i in range(4):
@@ -163,49 +158,60 @@
             device_id_type=MESH,
         )
 
-    def wind_copy(k, level):
-        return remote(own.at[pl.ds(0, 3)], winds.at[level], wind_sem, (k,), (peers[k], la, lo))
+    def wind_copies(k, level):
+        return [
+            remote(field.at[0], winds.at[level, f], wind_sem, (f, k), (peers[k], la, lo))
+            for f, field in enumerate((up, east, north))
+        ]
 
     for k in range(groups - 1):
-        wind_copy(k, g).start()
+        for copy in wind_copies(k, g):
+            copy.start()
 
     lane = lax.broadcasted_iota(jnp.int32, (own_tr, width), 1)
 
-    for i in range(4):
+    for i in range(8):
         loads[i].wait()
+    winds[g] = own[0:3]
 
     def turn(r, packed):
-        west, eastern = packed
+        done = []
+        hit = jnp.logical_or(lane == 2 * r, lane == lax.rem(2 * r + width - 1, width))
         for l in range(levels):
-            q = l * rows + r
-            tile = raw[pl.ds(q, own_tr, stride=levels * rows), :]
+            tile = raw[pl.ds(l * rows + r, own_tr, stride=levels * rows), :]
             cells[l, r + 1] = tile
-            hit = lane == q
-            west = jnp.where(hit, pltpu.roll(tile, q, 1), west)
-            eastern = jnp.where(hit, pltpu.roll(tile, q + 1, 1), eastern)
-        return west, eastern
+            done.append(jnp.where(hit, pltpu.roll(tile, 2 * r, 1), packed[l]))
+        return tuple(done)
 
     zero = jnp.zeros((own_tr, width), jnp.float32)
-    west, eastern = lax.fori_loop(0, rows, turn, (zero, zero))
-    packs[0] = eastern
-    packs[1] = west
+    for l, packed in enumerate(lax.fori_loop(0, rows, turn, (zero,) * levels)):
+        packs[l] = packed
+
+    mine = pl.ds(pl.multiple_of(g * own_tr, own_tr), own_tr)
+
+    def part_of(group):
+        return pl.ds(pl.multiple_of(group * own_tr, own_tr), own_tr)
+
+    def pack_copy(k, group):
+        return remote(
+            packs.at[peers[k]], edges.at[part_of(group)], pack_sem, (k,), (peers[k], la, lo)
+        )
+
+    for k in range(groups - 1):
+        pack_copy(k, g).start()
+    edges[mine, :] = packs[g]
     lon_copies = [
-        (has_e, has_w, remote(packs.at[0], sides.at[0], lon_sem, (0,), dev_e)),
-        (has_w, has_e, remote(packs.at[1], sides.at[1], lon_sem, (1,), dev_w)),
+        (has_e, has_w, remote(edges, edges_in.at[0], lon_sem, (0,), dev_e)),
+        (has_w, has_e, remote(edges, edges_in.at[1], lon_sem, (1,), dev_w)),
+    ]
+    side_copies = [
+        (has_e, has_w, remote(own.at[pl.ds(1, 3)], side_in.at[0], side_sem, (0,), dev_e)),
+        (has_w, has_e, remote(own.at[pl.ds(1, 3)], side_in.at[1], side_sem, (1,), dev_w)),
     ]
     lat_copies = [
         (has_n, has_s, remote(cells.at[:, rows], cells.at[:, 0], lat_sem, (0,), dev_n)),
         (has_s, has_n, remote(cells.at[:, 1], cells.at[:, rows + 1], lat_sem, (1,), dev_s)),
     ]
-    lonv_copies = [
-        (has_e, has_w, remote(own.at[pl.ds(2, 2)], side_vt.at[0], lonv_sem, (0,), dev_e)),
-        (has_w, has_e, remote(own.at[pl.ds(2, 2)], side_vt.at[1], lonv_sem, (1,), dev_w)),
-    ]
-    wind_u = winds.at[:, 1]
-    lonu_copies = [
-        (has_e, has_w, remote(wind_u, side_u.at[0], lonu_sem, (0,), dev_e)),
-        (has_w, has_e, remote(wind_u, side_u.at[1], lonu_sem, (1,), dev_w)),
-    ]
     rim_copies = [
         (has_n, has_s, remote(rim_out.at[0], rim_in.at[0], rim_sem, (0,), dev_n)),
         (has_s, has_n, remote(rim_out.at[1], rim_in.at[1], rim_sem, (1,), dev_s)),
@@ -224,14 +230,10 @@
         pl.when(which[0])(copies[1][2].start)
 
     start_lat(lat_copies, follows)
-    await_answer(3)
-    pl.when(has_e)(lon_copies[0][2].start)
-    await_answer(2)
-    pl.when(has_w)(lon_copies[1][2].start)
 
     for k in range(groups - 1):
-        wind_copy(k, lax.rem(g + groups - 1 - k, groups)).wait_recv()
-    start_all(lonu_copies)
+        for copy in wind_copies(k, lax.rem(g + groups - 1 - k, groups)):
+            copy.wait_recv()
     for l in range(levels):
         rim_out[0, l : l + 1, :] = winds[l, 2, rows - 1 : rows, :]
         rim_out[1, l : l + 1, :] = winds[l, 2, 0:1, :]
@@ -239,7 +241,6 @@
         rim_out[0, levels + j : levels + j + 1, :] = own[1 + j, rows - 1 : rows, :]
         rim_out[1, levels + j : levels + j + 1, :] = own[1 + j, 0:1, :]
     start_lat(rim_copies, follows)
-    start_all(lonv_copies)
 
     row_at = lax.broadcasted_iota(jnp.int32, (rows, width), 0)
     lane_at = lax.broadcasted_iota(jnp.int32, (rows, width), 1)
@@ -261,8 +262,8 @@
     def zonal_vertical():
         for l in range(levels):
             u = winds[l, 1]
-            a_e = 0.5 * (u + from_east(u, side_u[1, l]))
-            a_w = 0.5 * (from_west(u, side_u[0, l]) + u)
+            a_e = jnp.where(lane_at < width - 1, 0.5 * (u + pltpu.roll(u, width - 1, 1)), 0.0)
+            a_w = jnp.where(lane_at > 0, 0.5 * (pltpu.roll(u, 1, 1) + u), 0.0)
             keep = 1.0 - jnp.maximum(a_e, 0.0) + jnp.minimum(a_w, 0.0)
             coef[1, l] = -jnp.minimum(a_e, 0.0)
             coef[2, l] = jnp.maximum(a_w, 0.0)
@@ -285,22 +286,17 @@
             coef[4, l] = jnp.maximum(a_s, 0.0)
             coef[0, l] = coef[7, l] - jnp.maximum(a_n, 0.0) + jnp.minimum(a_s, 0.0)
 
-    receive_all(lonu_copies)
     zonal_vertical()
     meridional(lambda l: winds[l, 2, 0:1, :], lambda l: winds[l, 2, 0:1, :])
-    receive_all(lon_copies)
-
     def first_row(i):
         odd = i % 2
         half = i // 2
         middle = pieces // 2
         return 2 * (odd * (middle + half) + (1 - odd) * (middle - 1 - half))
 
-    mine = pl.ds(pl.multiple_of(g * own_tr, own_tr), own_tr)
-
     def forward_copy(i, k, part):
         r0 = first_row(i)
-        part = pl.ds(pl.multiple_of(part * own_tr, own_tr), own_tr)
+        part = part_of(part)
         return remote(
             adv.at[peers[k], pl.ds(r0, 2)],
             block.at[pl.ds(r0, 2), part],
@@ -314,22 +310,13 @@
         for rr in range(2):
             r = r0 + rr
             for l in range(levels):
-                q = l * rows + r
 
                 def c(j):
                     return coef[j, l, pl.ds(r, 1), :]
 
                 here = cells[l, r + 1]
-                east_of = jnp.where(
-                    lane == width - 1,
-                    pltpu.roll(sides[1], width - 1 - q, 1),
-                    pltpu.roll(here, width - 1, 1),
-                )
-                west_of = jnp.where(
-                    lane == 0,
-                    pltpu.roll(sides[0], lax.rem(width - q, width), 1),
-                    pltpu.roll(here, 1, 1),
-                )
+                east_of = pltpu.roll(here, width - 1, 1)
+                west_of = pltpu.roll(here, 1, 1)
                 total = c(0) * here + c(1) * east_of + c(2) * west_of
                 total = total + c(3) * cells[l, r + 2] + c(4) * cells[l, r]
                 if l < levels - 1:
@@ -342,7 +329,18 @@
             forward_copy(i, k, g).start()
         return carry
 
-    lax.fori_loop(0, pieces - 2, advect, 0)
+    lax.fori_loop(0, 2, advect, 0)
+
+    for k in range(groups - 1):
+        pack_copy(k, lax.rem(g + groups - 1 - k, groups)).wait_recv()
+    await_answer(3)
+    pl.when(has_e)(side_copies[0][2].start)
+    pl.when(has_e)(lon_copies[0][2].start)
+    await_answer(2)
+    pl.when(has_w)(side_copies[1][2].start)
+    pl.when(has_w)(lon_copies[1][2].start)
+
+    lax.fori_loop(2, pieces - 2, advect, 0)
 
     await_answer(0)
     await_answer(1)
@@ -356,7 +354,7 @@
 
     def back_copy(i, k, level):
         r0 = first_row(i)
-        part = pl.ds(pl.multiple_of(peers[k] * own_tr, own_tr), own_tr)
+        part = part_of(peers[k])
         return remote(
             reacted.at[pl.ds(r0, 2), part],
             back.at[level, pl.ds(r0, 2)],
@@ -364,6 +362,22 @@
             (i, k),
             (peers[k], la, lo),
         )
+
+    receive_all(side_copies)
+    u = own[1]
+    a_w = 0.5 * (from_west(u, side_in[0, 0]) + u)
+    a_e = 0.5 * (u + from_east(u, side_in[1, 0]))
+    a_w = jnp.where(lane_at == 2 * row_at, a_w[:, 0:1], 0.0)
+    a_e = jnp.where(lane_at == lax.rem(2 * row_at + width - 1, width), a_e[:, width - 1 :], 0.0)
+    a = jnp.sum(a_w + a_e, axis=0, keepdims=True)
+    receive_all(lon_copies)
+    first_lane = lax.rem(lax.broadcasted_iota(jnp.int32, (species_all, width), 1), 2) == 0
+    beyond = jnp.where(
+        first_lane, pltpu.roll(edges_in[0], 1, 1), pltpu.roll(edges_in[1], width - 1, 1)
+    )
+    here = edges[...]
+    more, less = jnp.maximum(a, 0.0), jnp.minimum(a, 0.0)
+    fix[...] = jnp.where(first_lane, more * beyond + less * here, -(more * here + less * beyond))
 
     twice = (la + 1) * rows > 3 * lats * rows // 4
 
@@ -393,6 +407,12 @@
         def load(ref):
             return jnp.concatenate([ref[r0], ref[r0 + 1]], axis=1)
 
+        at_edge = lax.broadcasted_iota(jnp.int32, (species_all, width), 1)
+        at_edge = jnp.logical_or(at_edge == 0, at_edge == width - 1)
+        for r in (r0, r0 + 1):
+            moved = pltpu.roll(fix[...], lax.rem(width - 2 * r, width), 1)
+            block[r] = block[r] + jnp.where(at_edge, moved, 0.0)
+
         def keep(value):
             reacted[r0] = value[:, :width]
             reacted[r0 + 1] = value[:, width:]
@@ -411,27 +431,26 @@
             misc[3, pl.ds(r, 1), :] = jnp.sum(gain, axis=0, keepdims=True)
         return carry
 
-    lax.fori_loop(0, pieces // 2, react, 0)
+    lax.fori_loop(0, 3, react, 0)
 
     receive_all(rim_copies)
     receive_all(lat_copies)
     meridional(lambda l: rim_in[0, l : l + 1, :], lambda l: rim_in[1, l : l + 1, :])
     lax.fori_loop(pieces - 2, pieces, advect, 0)
 
-    lax.fori_loop(pieces // 2, pieces, react, 0)
-
-    receive_all(lonv_copies)
+    lax.fori_loop(3, pieces, react, 0)
+
 
     def around(f, j, west_tile, east_tile):
         s, n = rim_in[0, levels + j : levels + j + 1, :], rim_in[1, levels + j : levels + j + 1, :]
         return from_east(f, east_tile), from_west(f, west_tile), from_north(f, n), from_south(f, s)
 
-    t_e, t_w, t_n, t_s = around(t, 2, side_vt[0, 1], side_vt[1, 1])
+    t_e, t_w, t_n, t_s = around(t, 2, side_in[0, 2], side_in[1, 2])
     u = own[1]
-    e, w, n, s = around(u, 0, side_u[0, g], side_u[1, g])
+    e, w, n, s = around(u, 0, side_in[0, 0], side_in[1, 0])
     east_out[0] = u + diffusion * (e + w + n + s - 4.0 * u) - pressure * (t_e - t_w)
     v = own[2]
-    e, w, n, s = around(v, 1, side_vt[0, 0], side_vt[1, 0])
+    e, w, n, s = around(v, 1, side_in[0, 1], side_in[1, 1])
     north_out[0] = v + diffusion * (e + w + n + s - 4.0 * v) - pressure * (t_n - t_s)
     misc[2] = t + diffusion * (t_e + t_w + t_n + t_s - 4.0 * t)
 
@@ -450,10 +469,12 @@
 
     lax.fori_loop(0, pieces, collect, 0)
 
-    for sends, _, copy in lon_copies + lat_copies + lonv_copies + lonu_copies + rim_copies:
+    for sends, _, copy in lon_copies + lat_copies + side_copies + rim_copies:
         pl.when(sends)(copy.wait_send)
     for k in range(groups - 1):
-        wind_copy(k, g).wait_send()
+        for copy in wind_copies(k, g):
+            copy.wait_send()
+        pack_copy(k, g).wait_send()
 
     def finish(i, carry):
         for k in range(groups - 1):
@@ -504,16 +525,17 @@
         scratch_shapes=[
             pltpu.VMEM((own_tr * levels * rows, width), f32),
             pltpu.VMEM((levels, rows + 2, own_tr, width), f32),
-            pltpu.VMEM((2, own_tr, width), f32),
-            pltpu.VMEM((2, own_tr, width), f32),
+            pltpu.VMEM((levels, own_tr, width), f32),
+            pltpu.VMEM((all_tr, width), f32),
+            pltpu.VMEM((2, all_tr, width), f32),
+            pltpu.VMEM((all_tr, width), f32),
             pltpu.VMEM((levels, rows, own_tr, width), f32),
             pltpu.VMEM((rows, all_tr, width), f32),
             pltpu.VMEM((rows, all_tr, width), f32),
             pltpu.VMEM((levels, rows, own_tr, width), f32),
             pltpu.VMEM((4, rows, width), f32),
             pltpu.VMEM((levels, 3, rows, width), f32),
-            pltpu.VMEM((2, levels, rows, width), f32),
-            pltpu.VMEM((2, 2, rows, width), f32),
+            pltpu.VMEM((2, 3, rows, width), f32),
             pltpu.VMEM((2, 8, width), f32),
             pltpu.VMEM((2, 8, width), f32),
             pltpu.VMEM((8, levels, rows, width), f32),
@@ -524,10 +546,10 @@
             pltpu.VMEM((1, all_tr), f32),
             pltpu.VMEM((all_tr, all_tr), f32),
             dma((13,)),
-            dma((2, groups - 1)),
+            dma((2, 3, groups - 1)),
             dma((2, 2)),
             dma((2, 2)),
-            dma((2, 2)),
+            dma((2, groups - 1)),
             dma((2, 2)),
             dma((2, 2)),
             dma((2, pieces, groups - 1)),

time: 41.3 us -> 37.2 us (0.901)
  Pallas kernels: 40.5 us -> 36.5 us
    pallas_call x1, Pallas kernels: 39.5 us -> 35.4 us  [local(): pl.pallas_call(functools.partial(kernel, sizes), out_shape=(pltpu.VMEM((o...]
where the time goes in v3:
time: 37.2 us; the launch traced here: 37.1 us
  Pallas kernels  36.5 us (98%)
  between operations  0.64 us (2%)
    pallas_call x1, Pallas kernels, local(): pl.pallas_call(functools.partial(kernel, sizes), out_shape=(pltpu.VMEM((o...  35.4 us
    pallas_call x1, Pallas kernels, local(): pl.pallas_call(store, out_shape=tuple((jax.ShapeDtypeStruct(x.shape, f32)...  1.03 us

profile of v3, /device:TPU:1, one launch (start us, length us, event | category | flops | bytes accessed | tf_op | source)
XLA Modules:
  0.0 37.1 jit_solution(2949555108807399525)
XLA Ops:
  0.6 35.4 %couple.1 = (f32[2048,128]{1,0:T(8,128)S(1)}, f32[1,16,128]{2,1,0:T(8,128)S(1)}, f32[1,16,128]{2,1,0:T(8,128)S(1)}, f32[1,16,128]{2,1,0:T(8,128)S(1)}) custom-call(f32[2048,128]{1,0:T(8,128)} %bitcast.3, f32[1,16,128]{2,1,0:T(8,128)} %east.1, f32[1,16,128]{2,1,0:T(8,128)} %north.1, f32[1,16,128]{2,1,0:T(8,128)} %up.1, f32[1,16,128]{2,1,0:T(8,128)} %warm.1, ...), custom_call_target="tpu_custom_call" | custom-call | tf_op jit(solution)/shard_map/couple/pallas_call | solution.py:519
  36.1 1.0 %store.1 = (f32[2048,128]{1,0:T(8,128)}, f32[1,16,128]{2,1,0:T(8,128)}, f32[1,16,128]{2,1,0:T(8,128)}, f32[1,16,128]{2,1,0:T(8,128)}) custom-call(f32[2048,128]{1,0:T(8,128)S(1)} %get-tuple-element.12.tracers, f32[1,16,128]{2,1,0:T(8,128)S(1)} %get-tuple-element.13.east, f32[1,16,128]{2,1,0:T(8,128)S(1)} %get-tuple-element.14.north, ...), custom_call_target="tpu_custom_call" | custom-call | tf_op jit(solution)/shard_map/store/pallas_call | solution.py:566

commit v4 on v3

--- a/solution.py
+++ b/solution.py
@@ -69,6 +69,7 @@
     repeats = comp_v.shape[0] // species_all
     pieces = rows // 2
     peers = [lax.rem(g + k, groups) for k in range(1, groups)]
+    far_first = sorted(range(groups - 1), key=lambda k: -min(k + 1, groups - 1 - k))
     has_s, has_n, has_w, has_e = la > 0, la < lats - 1, lo > 0, lo < lons - 1
     dev_s, dev_n, dev_w, dev_e = (g, la - 1, lo), (g, la + 1, lo), (g, la, lo - 1), (g, la, lo + 1)
 
@@ -144,6 +145,8 @@
         edges_in[1] = jnp.zeros((species_all, width), jnp.float32)
         side_in[1] = jnp.zeros((3, rows, width), jnp.float32)
 
+    for i in range(4, 7):
+        loads[i].wait()
     pl.semaphore_wait(barrier, groups - 1 + sum(f.astype(jnp.int32) for f in follows))
     for i in range(4):
         pl.when(follows[i])(functools.partial(answer, i))
@@ -160,17 +163,17 @@
 
     def wind_copies(k, level):
         return [
-            remote(field.at[0], winds.at[level, f], wind_sem, (f, k), (peers[k], la, lo))
-            for f, field in enumerate((up, east, north))
+            remote(own.at[f], winds.at[level, f], wind_sem, (f, k), (peers[k], la, lo))
+            for f in range(3)
         ]
 
-    for k in range(groups - 1):
+    for k in far_first:
         for copy in wind_copies(k, g):
             copy.start()
 
     lane = lax.broadcasted_iota(jnp.int32, (own_tr, width), 1)
 
-    for i in range(8):
+    for i in (0, 1, 2, 3, 7):
         loads[i].wait()
     winds[g] = own[0:3]
 
@@ -197,7 +200,7 @@
             packs.at[peers[k]], edges.at[part_of(group)], pack_sem, (k,), (peers[k], la, lo)
         )
 
-    for k in range(groups - 1):
+    for k in far_first:
         pack_copy(k, g).start()
     edges[mine, :] = packs[g]
     lon_copies = [
@@ -325,7 +328,7 @@
                     total = total + c(6) * cells[l - 1, r + 1]
                 adv[l, r] = total
             block[r, mine, :] = adv[g, r]
-        for k in range(groups - 1):
+        for k in far_first:
             forward_copy(i, k, g).start()
         return carry
 
@@ -423,7 +426,7 @@
         def _():
             keep(substep(load(reacted), 1))
 
-        for k in range(groups - 1):
+        for k in far_first:
             back_copy(i, k, g).start()
         for rr in range(2):
             r = r0 + rr
@@ -431,14 +434,16 @@
             misc[3, pl.ds(r, 1), :] = jnp.sum(gain, axis=0, keepdims=True)
         return carry
 
-    lax.fori_loop(0, 3, react, 0)
+    far = jnp.logical_or(jnp.logical_and(lax.rem(la, 4) == 3, has_n), jnp.logical_and(lax.rem(la, 4) == 0, has_s))
+    early = jnp.where(far, 3, 0)
+    lax.fori_loop(0, early, react, 0)
 
     receive_all(rim_copies)
     receive_all(lat_copies)
     meridional(lambda l: rim_in[0, l : l + 1, :], lambda l: rim_in[1, l : l + 1, :])
     lax.fori_loop(pieces - 2, pieces, advect, 0)
 
-    lax.fori_loop(3, pieces, react, 0)
+    lax.fori_loop(early, pieces, react, 0)
 
 
     def around(f, j, west_tile, east_tile):
@@ -456,19 +461,6 @@
 
     temp_out[0] = misc[2] + misc[3] / misc[0]
 
-    def collect(i, carry):
-        r0 = first_row(i)
-        for k in range(groups - 1):
-            back_copy(i, k, lax.rem(g + groups - 1 - k, groups)).wait_recv()
-        for rr in range(2):
-            back[g, r0 + rr] = reacted[r0 + rr, mine, :]
-            for l in range(levels):
-                at = l * rows + r0 + rr
-                tracers[pl.ds(at, own_tr, stride=levels * rows), :] = back[l, r0 + rr]
-        return carry
-
-    lax.fori_loop(0, pieces, collect, 0)
-
     for sends, _, copy in lon_copies + lat_copies + side_copies + rim_copies:
         pl.when(sends)(copy.wait_send)
     for k in range(groups - 1):
@@ -476,13 +468,22 @@
             copy.wait_send()
         pack_copy(k, g).wait_send()
 
-    def finish(i, carry):
+    def collect(i, carry):
+        r0 = first_row(i)
         for k in range(groups - 1):
             forward_copy(i, k, g).wait_send()
             back_copy(i, k, g).wait_send()
+        for rr in range(2):
+            back[g, r0 + rr] = reacted[r0 + rr, mine, :]
+        for k in range(groups - 1):
+            back_copy(i, k, lax.rem(g + groups - 1 - k, groups)).wait_recv()
+        for rr in range(2):
+            for l in range(levels):
+                at = l * rows + r0 + rr
+                tracers[pl.ds(at, own_tr, stride=levels * rows), :] = back[l, r0 + rr]
         return carry
 
-    lax.fori_loop(0, pieces, finish, 0)
+    lax.fori_loop(0, pieces, collect, 0)
 
 
 def store(tracers, east, north, temp, tracers_out, east_out, north_out, temp_out, sem):

time: 37.2 us -> 36.7 us (0.987)
  Pallas kernels: 36.5 us -> 35.8 us
    pallas_call x1, Pallas kernels: 35.4 us -> 34.7 us  [local(): pl.pallas_call(functools.partial(kernel, sizes), out_shape=(pltpu.VMEM((o...]
where the time goes in v4:
time: 36.7 us; the launch traced here: 36.4 us
  Pallas kernels  35.8 us (98%)
  between operations  0.64 us (2%)
    pallas_call x1, Pallas kernels, local(): pl.pallas_call(functools.partial(kernel, sizes), out_shape=(pltpu.VMEM((o...  34.7 us
    pallas_call x1, Pallas kernels, local(): pl.pallas_call(store, out_shape=tuple((jax.ShapeDtypeStruct(x.shape, f32)...  1.03 us

profile of v4, /device:TPU:1, one launch (start us, length us, event | category | flops | bytes accessed | tf_op | source)
XLA Modules:
  0.0 36.4 jit_solution(7124710645639894811)
XLA Ops:
  0.6 34.7 %couple.1 = (f32[2048,128]{1,0:T(8,128)S(1)}, f32[1,16,128]{2,1,0:T(8,128)S(1)}, f32[1,16,128]{2,1,0:T(8,128)S(1)}, f32[1,16,128]{2,1,0:T(8,128)S(1)}) custom-call(f32[2048,128]{1,0:T(8,128)} %bitcast.3, f32[1,16,128]{2,1,0:T(8,128)} %east.1, f32[1,16,128]{2,1,0:T(8,128)} %north.1, f32[1,16,128]{2,1,0:T(8,128)} %up.1, f32[1,16,128]{2,1,0:T(8,128)} %warm.1, ...), custom_call_target="tpu_custom_call" | custom-call | tf_op jit(solution)/shard_map/couple/pallas_call | solution.py:520
  35.4 1.0 %store.1 = (f32[2048,128]{1,0:T(8,128)}, f32[1,16,128]{2,1,0:T(8,128)}, f32[1,16,128]{2,1,0:T(8,128)}, f32[1,16,128]{2,1,0:T(8,128)}) custom-call(f32[2048,128]{1,0:T(8,128)S(1)} %get-tuple-element.12.tracers, f32[1,16,128]{2,1,0:T(8,128)S(1)} %get-tuple-element.13.east, f32[1,16,128]{2,1,0:T(8,128)S(1)} %get-tuple-element.14.north, ...), custom_call_target="tpu_custom_call" | custom-call | tf_op jit(solution)/shard_map/store/pallas_call | solution.py:567

commit v5 on v4

--- a/solution.py
+++ b/solution.py
@@ -137,12 +137,12 @@
 
     @pl.when(jnp.logical_not(has_w))
     def _():
-        edges_in[0] = jnp.zeros((species_all, width), jnp.float32)
+        edges_in[0] = jnp.zeros((groups, 8, width), jnp.float32)
         side_in[0] = jnp.zeros((3, rows, width), jnp.float32)
 
     @pl.when(jnp.logical_not(has_e))
     def _():
-        edges_in[1] = jnp.zeros((species_all, width), jnp.float32)
+        edges_in[1] = jnp.zeros((groups, 8, width), jnp.float32)
         side_in[1] = jnp.zeros((3, rows, width), jnp.float32)
 
     for i in range(4, 7):
@@ -187,8 +187,17 @@
         return tuple(done)
 
     zero = jnp.zeros((own_tr, width), jnp.float32)
+    folds = own_tr // 8
+    share = width // folds
+    lane8 = lax.broadcasted_iota(jnp.int32, (8, width), 1)
+    holder = lax.rem(lane8 + 1, width) // share
     for l, packed in enumerate(lax.fori_loop(0, rows, turn, (zero,) * levels)):
-        packs[l] = packed
+        folded = packed[0:8]
+        for n in range(1, folds):
+            folded = jnp.where(
+                holder == n, pltpu.roll(packed[8 * n : 8 * n + 8], share * n, 1), folded
+            )
+        packs[l] = folded
 
     mine = pl.ds(pl.multiple_of(g * own_tr, own_tr), own_tr)
 
@@ -197,12 +206,12 @@
 
     def pack_copy(k, group):
         return remote(
-            packs.at[peers[k]], edges.at[part_of(group)], pack_sem, (k,), (peers[k], la, lo)
+            packs.at[peers[k]], edges.at[group], pack_sem, (k,), (peers[k], la, lo)
         )
 
     for k in far_first:
         pack_copy(k, g).start()
-    edges[mine, :] = packs[g]
+    edges[g] = packs[g]
     lon_copies = [
         (has_e, has_w, remote(edges, edges_in.at[0], lon_sem, (0,), dev_e)),
         (has_w, has_e, remote(edges, edges_in.at[1], lon_sem, (1,), dev_w)),
@@ -370,17 +379,23 @@
     u = own[1]
     a_w = 0.5 * (from_west(u, side_in[0, 0]) + u)
     a_e = 0.5 * (u + from_east(u, side_in[1, 0]))
-    a_w = jnp.where(lane_at == 2 * row_at, a_w[:, 0:1], 0.0)
-    a_e = jnp.where(lane_at == lax.rem(2 * row_at + width - 1, width), a_e[:, width - 1 :], 0.0)
+    a_w = jnp.where(lax.rem(lane_at, share) == 2 * row_at, a_w[:, 0:1], 0.0)
+    a_e = jnp.where(lax.rem(lane_at + 1, share) == 2 * row_at, a_e[:, width - 1 :], 0.0)
     a = jnp.sum(a_w + a_e, axis=0, keepdims=True)
     receive_all(lon_copies)
-    first_lane = lax.rem(lax.broadcasted_iota(jnp.int32, (species_all, width), 1), 2) == 0
-    beyond = jnp.where(
-        first_lane, pltpu.roll(edges_in[0], 1, 1), pltpu.roll(edges_in[1], width - 1, 1)
-    )
-    here = edges[...]
+    first_lane = lax.rem(lane8, 2) == 0
     more, less = jnp.maximum(a, 0.0), jnp.minimum(a, 0.0)
-    fix[...] = jnp.where(first_lane, more * beyond + less * here, -(more * here + less * beyond))
+    for n in range(groups):
+        beyond = jnp.where(
+            first_lane, pltpu.roll(edges_in[0, n], 1, 1), pltpu.roll(edges_in[1, n], width - 1, 1)
+        )
+        here = edges[n]
+        folded = jnp.where(
+            first_lane, more * beyond + less * here, -(more * here + less * beyond)
+        )
+        for m in range(folds):
+            at = n * own_tr + 8 * m
+            fix[at : at + 8, :] = pltpu.roll(folded, (width - share * m) % width, 1)
 
     twice = (la + 1) * rows > 3 * lats * rows // 4
 
@@ -526,9 +541,9 @@
         scratch_shapes=[
             pltpu.VMEM((own_tr * levels * rows, width), f32),
             pltpu.VMEM((levels, rows + 2, own_tr, width), f32),
-            pltpu.VMEM((levels, own_tr, width), f32),
-            pltpu.VMEM((all_tr, width), f32),
-            pltpu.VMEM((2, all_tr, width), f32),
+            pltpu.VMEM((levels, 8, width), f32),
+            pltpu.VMEM((groups, 8, width), f32),
+            pltpu.VMEM((2, groups, 8, width), f32),
             pltpu.VMEM((all_tr, width), f32),
             pltpu.VMEM((levels, rows, own_tr, width), f32),
             pltpu.VMEM((rows, all_tr, width), f32),

time: 36.7 us -> 36.5 us (level)
  the two profiles are of different devices: /device:TPU:1 before, /device:TPU:352 now
where the time goes in v5:
time: 36.5 us; the launch traced here: 36.4 us
  Pallas kernels  35.7 us (98%)
  between operations  0.64 us (2%)
    pallas_call x1, Pallas kernels, local(): pl.pallas_call(functools.partial(kernel, sizes), out_shape=(pltpu.VMEM((o...  34.7 us
    pallas_call x1, Pallas kernels, local(): pl.pallas_call(store, out_shape=tuple((jax.ShapeDtypeStruct(x.shape, f32)...  1.03 us

profile of v5, /device:TPU:352, one launch (start us, length us, event | category | flops | bytes accessed | tf_op | source)
XLA Modules:
  0.0 36.4 jit_solution(1407187102848299093)
XLA Ops:
  0.6 34.7 %couple.1 = (f32[2048,128]{1,0:T(8,128)S(1)}, f32[1,16,128]{2,1,0:T(8,128)S(1)}, f32[1,16,128]{2,1,0:T(8,128)S(1)}, f32[1,16,128]{2,1,0:T(8,128)S(1)}) custom-call(f32[2048,128]{1,0:T(8,128)} %bitcast.3, f32[1,16,128]{2,1,0:T(8,128)} %east.1, f32[1,16,128]{2,1,0:T(8,128)} %north.1, f32[1,16,128]{2,1,0:T(8,128)} %up.1, f32[1,16,128]{2,1,0:T(8,128)} %warm.1, ...), custom_call_target="tpu_custom_call" | custom-call | tf_op jit(solution)/shard_map/couple/pallas_call | solution.py:535
  35.3 1.0 %store.1 = (f32[2048,128]{1,0:T(8,128)}, f32[1,16,128]{2,1,0:T(8,128)}, f32[1,16,128]{2,1,0:T(8,128)}, f32[1,16,128]{2,1,0:T(8,128)}) custom-call(f32[2048,128]{1,0:T(8,128)S(1)} %get-tuple-element.12.tracers, f32[1,16,128]{2,1,0:T(8,128)S(1)} %get-tuple-element.13.east, f32[1,16,128]{2,1,0:T(8,128)S(1)} %get-tuple-element.14.north, ...), custom_call_target="tpu_custom_call" | custom-call | tf_op jit(solution)/shard_map/store/pallas_call | solution.py:582
